TPU v7x, 32 devices: a whole 2x2x4 slice. The times are simulated.
32 devices in a mesh: seq: 8 (over y, x, core), tp: 4 (over z).
Axes of the slice: x: 2, y: 2, z: 4, core: 2. Of those that a mesh axis runs over, the one named last changes fastest.
Arguments:
- layer_in: bfloat16 [2, 2048, 2048], P(None, 'seq'), may hold values from -6 to 6
- attn_gain: float32 [2048], replicated, may hold values from 0.1 to 1.9
- query_down: bfloat16 [2048, 1024], replicated, may hold values from -0.125 to 0.125
- latent_gain: float32 [1024], replicated, may hold values from 0.1 to 1.9
- query_up: bfloat16 [1024, 4096], P(None, 'tp'), may hold values from -0.1875 to 0.1875
- key_value: bfloat16 [2048, 512], replicated, may hold values from -0.125 to 0.125
- attn_out: bfloat16 [4096, 2048], P('tp'), may hold values from -1.5 to 1.5
- ffn_gain: float32 [2048], replicated, may hold values from 0.1 to 1.9
- gate_proj: bfloat16 [2048, 5632], P(None, 'tp'), may hold values from -0.125 to 0.125
- up_proj: bfloat16 [2048, 5632], P(None, 'tp'), may hold values from -0.125 to 0.125
- down_proj: bfloat16 [5632, 2048], P('tp'), may hold values from -0.078125 to 0.078125
- out_grad: bfloat16 [2, 2048, 2048], P(None, 'seq'), may hold values from -6 to 6
- doc_lengths: int32 [2, 8], replicated, may hold values from 1 to 1536, 2048 in all within a row
Outputs:
- layer_out: bfloat16 [2, 2048, 2048], P(None, 'seq')
- input_grad: bfloat16 [2, 2048, 2048], P(None, 'seq')
- attn_gain_grad: float32 [2048], P('seq')
- query_down_grad: float32 [2048, 1024], P('seq')
- latent_gain_grad: float32 [1024], P('seq')
- query_up_grad: float32 [1024, 4096], P('seq', 'tp')
- key_value_grad: float32 [2048, 512], P('seq')
- attn_out_grad: float32 [4096, 2048], P('tp', 'seq')
- ffn_gain_grad: float32 [2048], P('seq')
- gate_proj_grad: float32 [2048, 5632], P('seq', 'tp')
- up_proj_grad: float32 [2048, 5632], P('seq', 'tp')
- down_proj_grad: float32 [5632, 2048], P('tp', 'seq')
Inputs may be any that keep to these rules, and one draw needn't show every extreme that they name: `doc_lengths`: in each row the 8 lengths add up to 2048, and the longest is exactly 1536.
All inputs are finite; a program needn't handle non-finite values.
Results may differ from a plain program's by a relative error of at most 0.019.
Values may be sent and summed in bfloat16 or wider, within the bound.
No kernel may reach another device: no remote copies, remote signals or barrier semaphores. Data moves between devices by JAX's collectives and lax.ppermute only.
A program may use at most 256 MiB of HBM per device.

v0:
```python
import jax
import jax.numpy as jnp
from jax import lax
from jax.sharding import PartitionSpec as P

HD = 256


EPS = 1e-05
ROPE_BASE = 10000.0
NEG_FILL = -1e30


def matmul(left, right):
    return jnp.dot(left, right, preferred_element_type=jnp.float32)


def dot_rows(left, right):
    return lax.dot_general(
        left, right, (((0,), (0,)), ((), ())), preferred_element_type=jnp.float32
    )


def dot_cols(left, right):
    return lax.dot_general(
        left, right, (((1,), (1,)), ((), ())), preferred_element_type=jnp.float32
    )


def rms_forward(values, gain_vec):
    inv_rms = lax.rsqrt(jnp.mean(values * values, axis=-1, keepdims=True) + EPS)
    unit_rows = values * inv_rms
    return (unit_rows * gain_vec, unit_rows, inv_rms)


def rms_backward(grad_out, unit_rows, inv_rms, gain_vec):
    scaled = grad_out * gain_vec
    return inv_rms * (scaled - unit_rows * jnp.mean(scaled * unit_rows, axis=-1, keepdims=True))


def doc_layout(lengths, places):
    doc_ends = jnp.cumsum(lengths)
    starts = doc_ends - lengths
    owners = jnp.sum((places[:, None] >= doc_ends[None, :]).astype(jnp.int32), axis=1)
    member = owners[:, None] == jnp.arange(lengths.shape[0], dtype=jnp.int32)[None, :]
    inner_pos = places - jnp.sum(jnp.where(member, starts[None, :], 0), axis=1)
    return (owners, inner_pos)


def rotate(values, inner_pos, direction):
    half_dim = values.shape[-1] // 2
    frequency = ROPE_BASE ** (-jnp.arange(half_dim, dtype=jnp.float32) / half_dim)
    angles = inner_pos.astype(jnp.float32)[..., None] * frequency
    for padding_axis in range(values.ndim - 1 - angles.ndim + 1):
        angles = angles[..., None, :]
    cosine = jnp.cos(angles)
    sine_part = jnp.sin(angles) * direction
    front_half = values[..., :half_dim]
    back_half = values[..., half_dim:]
    return jnp.concatenate(
        [front_half * cosine - back_half * sine_part, back_half * cosine + front_half * sine_part],
        axis=-1,
    )


def key_scores(query_rows, key_piece, query_owner, query_place, lengths):
    count = key_piece.shape[1]
    key_places = jnp.arange(count, dtype=jnp.int32)

    def owner_rows(lengths_row):
        return doc_layout(lengths_row, key_places)[0]

    key_owner = jax.vmap(owner_rows)(lengths)
    scores = jnp.einsum(
        "rqd,rkd->rqk", query_rows, key_piece[..., :HD], preferred_element_type=jnp.float32
    ) * HD ** (-0.5)
    allowed = (query_owner[:, :, None] == key_owner[:, None, :]) & (
        key_places[None, None, :] <= query_place[None, :, None]
    )
    return (jnp.where(allowed, scores, NEG_FILL), allowed)


def forward_fold(carry, key_piece, query_rows, query_owner, query_place, lengths):
    row_peak, row_total, context = carry
    scores, allowed = key_scores(query_rows, key_piece, query_owner, query_place, lengths)
    new_peak = jnp.maximum(row_peak, jnp.max(scores, axis=-1))
    expo_vals = jnp.where(allowed, jnp.exp(scores - new_peak[..., None]), 0.0)
    row_total = jnp.sum(expo_vals, axis=-1)
    context = jnp.einsum(
        "rqk,rkd->rqd",
        expo_vals.astype(jnp.bfloat16),
        key_piece[..., HD:],
        preferred_element_type=jnp.float32,
    )
    return (new_peak, row_total, context)


def backward_fold(
    key_piece, query_rows, query_owner, query_place, lengths, log_total, context_rows, row_delta
):
    scores, allowed = key_scores(query_rows, key_piece, query_owner, query_place, lengths)
    probs = jnp.where(allowed, jnp.exp(scores - log_total[..., None]), 0.0)
    dprobs = jnp.einsum(
        "rqd,rkd->rqk", context_rows, key_piece[..., HD:], preferred_element_type=jnp.float32
    )
    dscores = (probs * (dprobs - row_delta[..., None])).astype(jnp.bfloat16)
    dquery = jnp.einsum(
        "rqk,rkd->rqd", dscores, key_piece[..., :HD], preferred_element_type=jnp.float32
    )
    dkeys = jnp.einsum(
        "rqk,rqd->rkd", dscores, query_rows, preferred_element_type=jnp.float32
    ) * HD ** (-0.5)
    dvalues = jnp.einsum(
        "rqk,rqd->rkd", probs.astype(jnp.bfloat16), context_rows, preferred_element_type=jnp.float32
    )
    update = jnp.concatenate([dkeys, dvalues], axis=-1)
    return (dquery, update)


def key_backward(kv_delta, inner_pos):
    turned = rotate(kv_delta[..., :HD], inner_pos, -1.0)
    return jnp.concatenate([turned, kv_delta[..., HD:]], axis=-1).astype(jnp.bfloat16)


def shards(
    layer_in,
    attn_gain,
    query_down,
    latent_gain,
    query_up,
    key_value,
    attn_out,
    ffn_gain,
    gate_proj,
    up_proj,
    down_proj,
    out_grad,
    doc_lengths,
):
    row_count, row_tokens, model_dim = layer_in.shape
    shard_index = lax.axis_index("seq")
    local_heads = query_up.shape[1] // HD
    tokens = row_count * row_tokens
    query_count = local_heads * row_tokens
    places = shard_index * row_tokens + jnp.arange(row_tokens, dtype=jnp.int32)

    def layout_row(lengths_row):
        return doc_layout(lengths_row, places)

    owners, inner_pos = jax.vmap(layout_row)(doc_lengths)
    stream = layer_in.astype(jnp.float32).reshape(tokens, model_dim)
    normed_full, unit_first, inv_first = rms_forward(stream, attn_gain)
    normed = normed_full.astype(jnp.bfloat16)
    latent = matmul(normed, query_down)
    latent_full, unit_latent, inv_latent = rms_forward(latent, latent_gain)
    latent_norm = latent_full.astype(jnp.bfloat16)
    raw_query = matmul(latent_norm, query_up).reshape(row_count, row_tokens, local_heads, HD)
    queries = rotate(raw_query, inner_pos, 1.0).astype(jnp.bfloat16)
    query_rows = queries.transpose(0, 2, 1, 3).reshape(row_count, query_count, HD)
    query_owner = jnp.tile(owners, (1, local_heads))
    query_place = jnp.tile(places, local_heads)
    kv_proj = matmul(normed, key_value).reshape(row_count, row_tokens, 2 * HD)
    key_part = rotate(kv_proj[..., :HD], inner_pos, 1.0)
    kv_shard = jnp.concatenate([key_part, kv_proj[..., HD:]], axis=-1).astype(jnp.bfloat16)
    start_carry = (
        jnp.full((row_count, query_count), NEG_FILL, jnp.float32),
        jnp.zeros((row_count, query_count), jnp.float32),
        jnp.zeros((row_count, query_count, HD), jnp.float32),
    )
    row_peak, row_total, context = forward_fold(
        start_carry,
        lax.all_gather(kv_shard, "seq", axis=1, tiled=True),
        query_rows,
        query_owner,
        query_place,
        doc_lengths,
    )
    context = context / row_total[..., None]
    log_total = row_peak + jnp.log(row_total)
    context_low = context.astype(jnp.bfloat16)
    context_flat = (
        context_low.reshape(row_count, local_heads, row_tokens, HD)
        .transpose(0, 2, 1, 3)
        .reshape(tokens, local_heads * HD)
    )
    attn_total = lax.psum(matmul(context_flat, attn_out), "tp")
    middle = stream + attn_total
    second_full, unit_second, inv_second = rms_forward(middle, ffn_gain)
    second_norm = second_full.astype(jnp.bfloat16)
    gate_act = matmul(second_norm, gate_proj)
    up_act = matmul(second_norm, up_proj)
    sigmoid_gate = jax.nn.sigmoid(gate_act)
    swish_gate = gate_act * sigmoid_gate
    hidden = (swish_gate * up_act).astype(jnp.bfloat16)
    ffn_total = lax.psum(matmul(hidden, down_proj), "tp")
    layer_out = (middle + ffn_total).astype(jnp.bfloat16).reshape(row_count, row_tokens, model_dim)
    grad_low = out_grad.reshape(tokens, model_dim)
    grad_full = grad_low.astype(jnp.float32)
    down_grad = dot_rows(hidden, grad_low)
    dhidden = dot_cols(grad_low, down_proj)
    gate_delta = (dhidden * up_act * sigmoid_gate * (1.0 + gate_act * (1.0 - sigmoid_gate))).astype(
        jnp.bfloat16
    )
    up_delta = (dhidden * swish_gate).astype(jnp.bfloat16)
    gate_grad = dot_rows(second_norm, gate_delta)
    upproj_grad = dot_rows(second_norm, up_delta)
    second_delta = lax.psum(dot_cols(gate_delta, gate_proj) + dot_cols(up_delta, up_proj), "tp")
    middle_delta = grad_full + rms_backward(second_delta, unit_second, inv_second, ffn_gain)
    middle_low = middle_delta.astype(jnp.bfloat16)
    mixer_grad = dot_rows(context_flat, middle_low)
    column_grads = (
        lax.psum_scatter(mixer_grad, "seq", scatter_dimension=1, tiled=True),
        lax.psum_scatter(down_grad, "seq", scatter_dimension=1, tiled=True),
    )
    context_delta = dot_cols(middle_low, attn_out).astype(jnp.bfloat16)
    context_rows = (
        context_delta.reshape(row_count, row_tokens, local_heads, HD)
        .transpose(0, 2, 1, 3)
        .reshape(row_count, query_count, HD)
    )
    row_delta = jnp.sum(context_rows.astype(jnp.float32) * context, axis=-1)
    dquery, key_deltas = backward_fold(
        lax.all_gather(kv_shard, "seq", axis=1, tiled=True),
        query_rows,
        query_owner,
        query_place,
        doc_lengths,
        log_total,
        context_rows,
        row_delta,
    )
    kv_part = lax.psum_scatter(key_deltas, "seq", scatter_dimension=1, tiled=True)
    dquery = dquery * HD ** (-0.5)
    query_delta = dquery.reshape(row_count, local_heads, row_tokens, HD).transpose(0, 2, 1, 3)
    query_low = (
        rotate(query_delta, inner_pos, -1.0).astype(jnp.bfloat16).reshape(tokens, local_heads * HD)
    )
    expand_grad = dot_rows(latent_norm, query_low)
    latent_part = dot_cols(query_low, query_up)
    latent_delta, kv_summed = lax.psum((latent_part, kv_part), "tp")
    kv_low = key_backward(kv_summed, inner_pos).reshape(tokens, 2 * HD)
    latent_back = rms_backward(latent_delta, unit_latent, inv_latent, latent_gain)
    latent_low = latent_back.astype(jnp.bfloat16)
    normed_delta = dot_cols(latent_low, query_down) + dot_cols(kv_low, key_value)
    input_grad = (
        (middle_delta + rms_backward(normed_delta, unit_first, inv_first, attn_gain))
        .astype(jnp.bfloat16)
        .reshape(row_count, row_tokens, model_dim)
    )
    gain_first = jnp.sum(normed_delta * unit_first, axis=0)
    gain_latent = jnp.sum(latent_delta * unit_latent, axis=0)
    gain_second = jnp.sum(second_delta * unit_second, axis=0)
    compress_grad = dot_rows(normed, latent_low)
    shared_grad = dot_rows(normed, kv_low)
    row_grads = (
        lax.psum_scatter(gain_first, "seq", scatter_dimension=0, tiled=True),
        lax.psum_scatter(compress_grad, "seq", scatter_dimension=0, tiled=True),
        lax.psum_scatter(gain_latent, "seq", scatter_dimension=0, tiled=True),
        lax.psum_scatter(expand_grad, "seq", scatter_dimension=0, tiled=True),
        lax.psum_scatter(shared_grad, "seq", scatter_dimension=0, tiled=True),
        lax.psum_scatter(gain_second, "seq", scatter_dimension=0, tiled=True),
        lax.psum_scatter(gate_grad, "seq", scatter_dimension=0, tiled=True),
        lax.psum_scatter(upproj_grad, "seq", scatter_dimension=0, tiled=True),
    )
    return (
        layer_out,
        input_grad,
        row_grads[0],
        row_grads[1],
        row_grads[2],
        row_grads[3],
        row_grads[4],
        column_grads[0],
        row_grads[5],
        row_grads[6],
        row_grads[7],
        column_grads[1],
    )


def solution(mesh):
    return jax.shard_map(
        shards,
        mesh=mesh,
        in_specs=(
            P(None, "seq", None),
            P(),
            P(),
            P(),
            P(None, "tp"),
            P(),
            P("tp", None),
            P(),
            P(None, "tp"),
            P(None, "tp"),
            P("tp", None),
            P(None, "seq", None),
            P(),
        ),
        out_specs=(
            P(None, "seq", None),
            P(None, "seq", None),
            P("seq"),
            P("seq", None),
            P("seq"),
            P("seq", "tp"),
            P("seq", None),
            P("tp", "seq"),
            P("seq"),
            P("seq", "tp"),
            P("seq", "tp"),
            P("tp", "seq"),
        ),
        check_vma=False,
    )
```

profile of v0, /device:TPU:0, one launch (start us, length us, event | category | flops | bytes accessed | tf_op | source)
XLA Modules:
  0.0 1362.6 jit_solution(8796911887741906710)
XLA Ops:
  11.2 2.9 fusion.24
  23.6 2.6 fusion.63
  26.2 3.7 reshape.210
  33.8 2.7 iota_compare_fusion
  36.5 20.0 %all-gather.2.cloned.1.call-done = bf16[2,2048,512]{2,1,0:T(8,128)(2,1)} async-done(((bf16[2,256,512]{2,1,0:T(8,128)(2,1)}), bf16[2,2048,512]{2,1,0:T(8,128)(2,1)}) %all-gather.2.cloned.1.call-update) | async-done | bytes 4194320 | tf_op jit(solution)/shard_map/all_gather | solution.py:172
  56.5 7.5 fusion.64
  64.6 6.1 fusion
  70.8 8.3 fusion.40
  82.4 4.4 fusion.65
  86.9 155.1 %all-reduce.9.cloned.1.call-done = f32[512,2048]{1,0:T(8,128)} async-done(((f32[512,2048]{1,0:T(8,128)}), f32[512,2048]{1,0:T(8,128)}) %all-reduce.9.cloned.1.call-update) | async-done | bytes 4194320 | tf_op jit(solution)/shard_map/psum | solution.py:186
  242.0 3.5 multiply_reduce_fusion.2
  246.0 10.1 fusion.67
  256.1 5.0 fusion.66
  261.2 8.2 multiply_convert_fusion.2
  269.4 4.9 fusion.69
  274.3 5.1 convolution_add_fusion.1
  280.1 153.5 %all-reduce.11.cloned.1.call-done = f32[512,2048]{1,0:T(8,128)} async-done(((f32[512,2048]{1,0:T(8,128)}), f32[512,2048]{1,0:T(8,128)}) %all-reduce.11.cloned.1.call-update) | async-done | bytes 4194320 | tf_op jit(solution)/shard_map/psum | solution.py:207
  433.6 4.6 multiply_reduce_fusion
  439.5 2.8 multiply_add_fusion
  444.3 3.3 convolution_convert_fusion
  452.4 12.0 fusion.3
  464.4 13.9 %multiply_convert_fusion = bf16[2,1024,2048]{2,1,0:T(8,128)(2,1)} fusion(f32[2,1024,2048]{2,1,0:T(8,128)} %copy-done.9, f32[2,1024]{1,0:T(2,128)S(1)} %multiply_reduce_fusion.5, f32[2,1024]{1,0:T(2,128)S(1)} %log_add_fusion, s32[2,2048]{1,0:T(2,128)S(1)} %convert_reduce_fusion, s32[2,1024]{1,0:T(2,128)S(1)} %bitcast.132, ...), kind=kOutput, calls=%fused_computation | convolution fusion | flops 2176843776 | bytes 30449664 | tf_op jit(solution)/shard_map/rqd,rkd->rqk/dot_general | solution.py:103
  478.3 6.9 convolution_multiply_fusion
  485.3 4.6 pad_maximum_fusion
  491.2 7.9 fusion.68
  499.1 7.2 fusion.34
  509.3 2.6 fusion.70
  512.0 48.4 %reduce-scatter.9.cloned.1.call-done = f32[2,256,512]{2,1,0:T(8,128)} async-done(((f32[2,2048,512]{2,1,0:T(8,128)}), f32[2,256,512]{2,1,0:T(8,128)}) %reduce-scatter.9.cloned.1.call-update) | async-done | bytes 1048592 | tf_op jit(solution)/shard_map/reduce_scatter | solution.py:232
  560.4 5.1 fusion.62
  566.7 8.0 fusion.37
  576.0 9.0 fusion.75
  586.4 7.8 fusion.74
  595.5 7.8 fusion.73
  603.3 217.7 %all-reduce.13.cloned.1.call-done = (f32[512,2048]{1,0:T(8,128)}, f32[512,1024]{1,0:T(8,128)}, f32[2,256,512]{2,1,0:T(8,128)}) async-done(((f32[512,2048]{1,0:T(8,128)}, f32[512,1024]{1,0:T(8,128)}, f32[2,256,512]{2,1,0:T(8,128)}), (f32[512,2048]{1,0:T(8,128)}, f32[512,1024]{1,0:T(8,128)}, f32[2,256,512]{2,1,0:T(8,128)})) %all-reduce.13.cloned.1.call-update) | async-done | bytes 7340048 | tf_op jit(solution)/shard_map/psum | solution.py:195
  824.9 4.9 fusion.56
  830.2 4.0 multiply_reduce_fusion.3
  835.4 5.7 fusion.72
  843.7 4.7 fusion.71
  848.4 3.8 fusion.19
  852.2 24.2 %all-reduce.3 = (f32[2048]{0:T(1024)S(1)}, f32[1024]{0:T(1024)S(1)}, f32[2048]{0:T(1024)S(1)}) all-reduce(f32[2048]{0:T(1024)S(1)} %get-tuple-element.14, f32[1024]{0:T(1024)S(1)} %copy-done.42, f32[2048]{0:T(1024)S(1)} %get-tuple-element.12), channel_id=3, replica_groups=mesh['seq'=8,'tp'=4] {'seq'}, use_global_device_ids=true, to_apply=%region_20.21.clone | all-reduce | flops 5120 | bytes 40960
  878.3 5.6 add_convert_fusion
  886.1 2.4 fusion.18
  888.6 62.4 %reduce-scatter.17.cloned.1.call-done = f32[1024,256]{1,0:T(8,128)} async-done(((f32[1024,2048]{1,0:T(8,128)}), f32[1024,256]{1,0:T(8,128)}) %reduce-scatter.17.cloned.1.call-update) | async-done | bytes 1048592 | tf_op jit(solution)/shard_map/reduce_scatter | solution.py:212
  950.9 91.3 %reduce-scatter.23.cloned.1.call-done = f32[1408,256]{1,0:T(8,128)} async-done(((f32[1408,2048]{1,0:T(8,128)}), f32[1408,256]{1,0:T(8,128)}) %reduce-scatter.23.cloned.1.call-update) | async-done | bytes 1441808 | tf_op jit(solution)/shard_map/reduce_scatter | solution.py:213
  1042.2 91.3 %reduce-scatter.21.cloned.1.call-done = f32[256,1408]{1,0:T(8,128)} async-done(((f32[2048,1408]{1,0:T(8,128)}), f32[256,1408]{1,0:T(8,128)}) %reduce-scatter.21.cloned.1.call-update) | async-done | bytes 1441808 | tf_op jit(solution)/shard_map/reduce_scatter | solution.py:263
  1133.5 91.1 %reduce-scatter.19.cloned.1.call-done = f32[256,1408]{1,0:T(8,128)} async-done(((f32[2048,1408]{1,0:T(8,128)}), f32[256,1408]{1,0:T(8,128)}) %reduce-scatter.19.cloned.1.call-update) | async-done | bytes 1441808 | tf_op jit(solution)/shard_map/reduce_scatter | solution.py:262
  1224.6 55.6 %reduce-scatter.15.cloned.1.call-done = f32[256,512]{1,0:T(8,128)} async-done(((f32[2048,512]{1,0:T(8,128)}), f32[256,512]{1,0:T(8,128)}) %reduce-scatter.15.cloned.1.call-update) | async-done | bytes 524304 | tf_op jit(solution)/shard_map/reduce_scatter | solution.py:260
  1280.3 75.2 %reduce-scatter.11.cloned.1.call-done = f32[256,1024]{1,0:T(8,128)} async-done(((f32[2048,1024]{1,0:T(8,128)}), f32[256,1024]{1,0:T(8,128)}) %reduce-scatter.11.cloned.1.call-update) | async-done | bytes 1048592 | tf_op jit(solution)/shard_map/reduce_scatter | solution.py:257
  (201 shorter events, 50.8 us)
Async XLA Ops:
  7.2 49.3 %all-gather.2.cloned.1.call-start = ((), (), s32[]{:S(2)}) async-start(), calls=%async_computation.8 | async-start | bytes 4718592 | tf_op jit(solution)/shard_map/all_gather | solution.py:172
  7.3 6.9 copy-start.43
  9.1 5.1 copy-start.40
  11.2 5.8 copy-start.33
  16.0 13.9 %copy-start.20 = (f32[2,256,128]{2,1,0:T(8,128)}, f32[2,256,128]{2,1,0:T(8,128)S(1)}, u32[]{:S(2)}) copy-start(f32[2,256,128]{2,1,0:T(8,128)S(1)} %get-tuple-element.41) | copy-start | bytes 786436
  16.9 225.0 %all-reduce.9.cloned.1.call-start = ((), (), s32[]{:S(2)}) async-start(), calls=%async_computation.9 | async-start | bytes 8388608 | tf_op jit(solution)/shard_map/psum | solution.py:186
  17.0 5.2 copy-start.37
  56.5 8.1 copy-start.14
  64.0 6.7 copy-start.9
  86.8 158.6 %copy-start.30 = (f32[2048]{0:T(1024)S(1)}, f32[2048]{0:T(1024)}, u32[]{:S(2)}) copy-start(f32[2048]{0:T(1024)} %param.20) | copy-start | bytes 24580
  86.9 346.7 %all-reduce.11.cloned.1.call-start = ((), (), s32[]{:S(2)}) async-start(), calls=%async_computation.10 | async-start | bytes 8388608 | tf_op jit(solution)/shard_map/psum | solution.py:207
  245.5 10.6 copy-start.1
  245.5 10.6 slice-start
  245.9 10.1 copy-start.22
  245.9 10.1 slice-start.1
  246.0 15.2 %slice-start.4 = ((s8[5767168]{0:T(1024)(128)(4,1)}), s8[4194304]{0:T(1024)(128)(4,1)S(1)}, s32[]{:S(2)}) async-start(s8[5767168]{0:T(1024)(128)(4,1)} %bitcast.141), calls=%async_computation.24 | async-start | bytes 8388608
  256.1 5.1 copy-start.23
  256.1 5.0 slice-start.5
  256.1 18.2 %slice-start.2 = ((s8[5767168]{0:T(1024)(128)(4,1)}), s8[4194304]{0:T(1024)(128)(4,1)S(1)}, s32[]{:S(2)}) async-start(s8[5767168]{0:T(1024)(128)(4,1)} %bitcast.139), calls=%async_computation.22 | async-start | bytes 8388608
  261.1 13.2 slice-start.3
  269.4 5.0 copy-start.55
  279.4 280.9 %reduce-scatter.9.cloned.1.call-start = ((), (), s32[]{:S(2)}) async-start(), calls=%async_computation.11 | async-start | bytes 9437184 | tf_op jit(solution)/shard_map/reduce_scatter | solution.py:232
  433.6 5.9 copy-start.10
  439.5 4.8 copy-start.46
  464.4 13.9 %copy-start.25 = (bf16[2,4,256,256]{3,2,1,0:T(8,128)(2,1)S(1)}, bf16[2,4,256,256]{3,2,1,0:T(8,128)(2,1)}, u32[]{:S(2)}) copy-start(bf16[2,4,256,256]{3,2,1,0:T(8,128)(2,1)} %copy.48) | copy-start | bytes 3145732
  478.3 7.0 copy-start.17
  489.9 331.1 %all-reduce.13.cloned.1.call-start = ((), (), s32[]{:S(2)}) async-start(), calls=%async_computation.19 | async-start | bytes 14680064 | tf_op jit(solution)/shard_map/psum | solution.py:195
  491.2 7.9 copy-start.48
  512.0 48.4 %copy-start.29 = (f32[1024]{0:T(1024)S(1)}, f32[1024]{0:T(1024)}, u32[]{:S(2)}) copy-start(f32[1024]{0:T(1024)} %param.16) | copy-start | bytes 12292
  512.0 48.4 %copy-start.32 = (f32[512]{0:T(512)S(1)}, f32[512]{0:T(512)}, u32[]{:S(2)}) copy-start(f32[512]{0:T(512)} %copy-done.31) | copy-start | bytes 6148
  560.3 328.2 %reduce-scatter.13.cloned.1.call-start = ((), (), s32[]{:S(2)}) async-start(), calls=%async_computation.13 | async-start | bytes 4718592 | tf_op jit(solution)/shard_map/reduce_scatter | solution.py:259
  565.5 385.4 %reduce-scatter.17.cloned.1.call-start = ((), (), s32[]{:S(2)}) async-start(), calls=%async_computation.15 | async-start | bytes 9437184 | tf_op jit(solution)/shard_map/reduce_scatter | solution.py:212
  574.7 467.5 %reduce-scatter.23.cloned.1.call-start = ((), (), s32[]{:S(2)}) async-start(), calls=%async_computation.18 | async-start | bytes 12976128 | tf_op jit(solution)/shard_map/reduce_scatter | solution.py:213
  585.0 548.5 %reduce-scatter.21.cloned.1.call-start = ((), (), s32[]{:S(2)}) async-start(), calls=%async_computation.17 | async-start | bytes 12976128 | tf_op jit(solution)/shard_map/reduce_scatter | solution.py:263
  594.1 630.5 %reduce-scatter.19.cloned.1.call-start = ((), (), s32[]{:S(2)}) async-start(), calls=%async_computation.16 | async-start | bytes 12976128 | tf_op jit(solution)/shard_map/reduce_scatter | solution.py:262
  603.2 218.8 %copy-start.41 = (f32[2,256]{1,0:T(2,128)S(1)}, f32[2,256]{1,0:T(2,128)}, u32[]{:S(2)}) copy-start(f32[2,256]{1,0:T(2,128)} %copy-done.40) | copy-start | bytes 6148
  603.2 218.8 %copy-start.44 = (f32[128]{0:T(128)S(1)}, f32[128]{0:T(128)}, u32[]{:S(2)}) copy-start(f32[128]{0:T(128)} %copy-done.43) | copy-start | bytes 1540
  603.3 677.0 %reduce-scatter.15.cloned.1.call-start = ((), (), s32[]{:S(2)}) async-start(), calls=%async_computation.14 | async-start | bytes 4718592 | tf_op jit(solution)/shard_map/reduce_scatter | solution.py:260
  829.9 525.6 %reduce-scatter.11.cloned.1.call-start = ((), (), s32[]{:S(2)}) async-start(), calls=%async_computation.12 | async-start | bytes 9437184 | tf_op jit(solution)/shard_map/reduce_scatter | solution.py:257
  830.2 5.2 copy-start.12
  843.6 4.8 copy-start.5
  843.6 4.8 copy-start.27
  843.6 4.8 copy-start.34
  843.7 4.8 copy-start.38
  848.4 35.5 %copy-start.39 = (f32[1,2,2,128]{3,1,2,0:T(2,128)S(1)}, f32[1,2,2,128]{3,1,2,0:T(2,128)}, u32[]{:S(2)}) copy-start(f32[1,2,2,128]{3,1,2,0:T(2,128)} %copy-done.37) | copy-start | bytes 6148
  878.3 5.6 copy-start.4
  878.3 5.6 copy-start.6
  878.3 7.8 copy-start.16
  (27 other events, 58.8 us)
Sparse Core Ops, SparseCore 0:
  17.1 39.3 all-gather.1
  87.0 154.9 all-reduce.8
  279.5 153.9 all-reduce.10
  490.0 70.2 reduce-scatter.8
  563.5 257.4 all-reduce.12
  825.1 50.4 reduce-scatter.12
  879.7 71.2 reduce-scatter.16
  955.4 86.7 reduce-scatter.22
  1046.7 86.7 reduce-scatter.20
  1137.8 86.7 reduce-scatter.18
  1228.9 51.2 reduce-scatter.14
  1284.2 71.2 reduce-scatter.10
where the time goes:
time: 1370 us; the launch traced here: 1360 us
  waiting for transfers between devices  1060 us (77%)
  matrix products  172 us (13%)
  other arithmetic  54.6 us (4%)
  local copies, waits for them, and re-layouts  32.7 us (2%)
  blocking collectives  24.2 us (2%)
  between operations  16.6 us (1%)
    psum x1, waiting for transfers between devices, shards(): ffn_total = lax.psum(matmul(hidden, down_proj), 'tp')  218 us
    psum x1, waiting for transfers between devices, shards(): attn_total = lax.psum(matmul(context_flat, attn_out), 'tp')  155 us
    psum x1, waiting for transfers between devices, shards(): lax.psum(dot_cols(gate_delta, gate_proj) + dot_cols(up_delta, up_proj), '...  153 us
    reduce_scatter x1, waiting for transfers between devices, shards(): lax.psum_scatter(upproj_grad, 'seq', scatter_dimension=0, tiled=True)  91.3 us
    reduce_scatter x1, waiting for transfers between devices, shards(): lax.psum_scatter(down_grad, 'seq', scatter_dimension=1, tiled=True)  91.3 us
    reduce_scatter x1, waiting for transfers between devices, shards(): lax.psum_scatter(gate_grad, 'seq', scatter_dimension=0, tiled=True)  91.1 us
    reduce_scatter x1, waiting for transfers between devices, shards(): lax.psum_scatter(compress_grad, 'seq', scatter_dimension=0, tiled=True)  75.2 us
    reduce_scatter x1, waiting for transfers between devices, shards(): lax.psum_scatter(mixer_grad, 'seq', scatter_dimension=1, tiled=True)  62.4 us
  transfers between devices with their start and end apart: 12, of which 11 were waited for; matrix products, arithmetic and copies ran while one was open for 8% of the time, Pallas kernels for 0%

commit v1 on v0

v1 whole, which is shorter than its diff:
```python
import jax
import jax.numpy as jnp
from jax import lax
from jax.sharding import PartitionSpec as P

HD = 256
EPS = 1e-05
ROPE_BASE = 10000.0
NEG_FILL = -1e30
BF = jnp.bfloat16
F32 = jnp.float32


def matmul(left, right):
    return jnp.dot(left, right, preferred_element_type=F32)


def dot_rows(left, right):
    return lax.dot_general(left, right, (((0,), (0,)), ((), ())), preferred_element_type=F32)


def dot_cols(left, right):
    return lax.dot_general(left, right, (((1,), (1,)), ((), ())), preferred_element_type=F32)


def unit_norm(values):
    inv_rms = lax.rsqrt(jnp.mean(values * values, axis=-1, keepdims=True) + EPS)
    return values * inv_rms, inv_rms


def rms_backward(grad_out, unit_rows, inv_rms, gain_vec):
    scaled = grad_out * gain_vec
    return inv_rms * (scaled - unit_rows * jnp.mean(scaled * unit_rows, axis=-1, keepdims=True))


def doc_layout(lengths, places):
    doc_ends = jnp.cumsum(lengths)
    starts = doc_ends - lengths
    owners = jnp.sum((places[:, None] >= doc_ends[None, :]).astype(jnp.int32), axis=1)
    member = owners[:, None] == jnp.arange(lengths.shape[0], dtype=jnp.int32)[None, :]
    inner_pos = places - jnp.sum(jnp.where(member, starts[None, :], 0), axis=1)
    return owners, inner_pos


def turn(values, cosine, sine):
    half = values.shape[-1] // 2
    front, back = values[..., :half], values[..., half:]
    return jnp.concatenate([front * cosine - back * sine, back * cosine + front * sine], axis=-1)


def build(n_seq, n_tp):
    seq_bits = n_seq.bit_length() - 1
    tp_bits = n_tp.bit_length() - 1

    def swap(value, axis, bit):
        count = n_seq if axis == "seq" else n_tp
        return lax.ppermute(value, axis, [(i, i ^ (1 << bit)) for i in range(count)])

    def pick(blocks, where, axis):
        return lax.dynamic_index_in_dim(blocks, where, axis, keepdims=False)

    def tp_scatter(part, me):
        tokens, width = part.shape
        held = part.astype(BF).reshape(n_tp, tokens // n_tp, width)
        for bit in range(tp_bits):
            mine = (me >> bit) & 1
            pairs = held.reshape(held.shape[0] // 2, 2, *held.shape[1:])
            got = swap(pick(pairs, 1 - mine, 1), "tp", bit)
            total = pick(pairs, mine, 1).astype(F32) + got.astype(F32)
            held = total if bit == tp_bits - 1 else total.astype(BF)
        return held[0]

    def tp_gather(block, me):
        held = block[None]
        for bit in reversed(range(tp_bits)):
            mine = (me >> bit) & 1
            got = swap(held, "tp", bit)
            low = jnp.where(mine == 0, held, got)
            high = jnp.where(mine == 0, got, held)
            held = jnp.stack([low, high], axis=1).reshape(-1, *block.shape)
        return held.reshape(-1, block.shape[-1])

    def seq_gather(block, order):
        have = {0: block}
        for bit in order:
            keys = sorted(have)
            got = swap(jnp.stack([have[k] for k in keys]), "seq", bit)
            for i, k in enumerate(keys):
                have[k | (1 << bit)] = got[i]
        return [have[r] for r in range(n_seq)]

    def halve(blocks, me_bits, bit, bits_left, last):
        axis = bits_left.index(bit)
        mine = me_bits[bit]
        got = swap(pick(blocks, 1 - mine, axis), "seq", bit)
        total = pick(blocks, mine, axis).astype(F32) + got.astype(F32)
        return total if last else total.astype(BF)

    def seq_finish(blocks, me_bits, left):
        rows = blocks.shape[len(left)]
        front = lax.slice_in_dim(blocks, 0, rows // 2, axis=len(left))
        back = lax.slice_in_dim(blocks, rows // 2, rows, axis=len(left))
        done = []
        for piece, order in ((front, sorted(left)), (back, sorted(left, reverse=True))):
            rest = list(left)
            for i, bit in enumerate(order):
                piece = halve(piece, me_bits, bit, rest, i == len(order) - 1)
                rest.remove(bit)
            done.append(piece)
        return jnp.concatenate(done, axis=0)

    def split_cols(acts, me_bits):
        tokens, width = acts.shape
        blocks = acts.reshape(tokens, n_seq // 2, 2, width // n_seq)
        return (
            pick(blocks, 1 - me_bits[0], 2).reshape(tokens, width // 2),
            pick(blocks, me_bits[0], 2).reshape(tokens, width // 2),
        )

    upper = list(reversed(range(1, seq_bits)))

    def grad_rows(acts_pair, deltas, me_bits):
        away, home = acts_pair
        got = swap(dot_rows(away, deltas).astype(BF), "seq", 0)
        kept = (dot_rows(home, deltas) + got.astype(F32)).astype(BF)
        rows = kept.shape[0] // (n_seq // 2)
        return seq_finish(kept.reshape([2] * len(upper) + [rows, kept.shape[1]]), me_bits, upper)

    def grad_cols(acts, deltas_pair, me_bits):
        away, home = deltas_pair
        got = swap(dot_rows(acts, away).astype(BF), "seq", 0)
        kept = (dot_rows(acts, home) + got.astype(F32)).astype(BF)
        cols = kept.shape[1] // (n_seq // 2)
        blocks = kept.reshape(kept.shape[0], n_seq // 2, cols).transpose(1, 0, 2)
        return seq_finish(blocks.reshape([2] * len(upper) + [kept.shape[0], cols]), me_bits, upper)

    def shards(
        layer_in, attn_gain, query_down, latent_gain, query_up, key_value, attn_out,
        ffn_gain, gate_proj, up_proj, down_proj, out_grad, doc_lengths,
    ):
        n_rows, length, model_dim = layer_in.shape
        seq_me = lax.axis_index("seq")
        tp_me = lax.axis_index("tp")
        me_bits = [(seq_me >> b) & 1 for b in range(seq_bits)]
        heads = query_up.shape[1] // HD
        block = length // n_tp
        scale = HD ** (-0.5)
        places = seq_me * length + jnp.arange(length, dtype=jnp.int32)
        key_places = jnp.concatenate(
            [(seq_me ^ r) * length + jnp.arange(length, dtype=jnp.int32) for r in range(n_seq)]
        )
        frequency = ROPE_BASE ** (-jnp.arange(HD // 2, dtype=F32) / (HD // 2))
        rows = range(n_rows)

        def own(full):
            return lax.dynamic_slice_in_dim(full, tp_me * block, block, 0)

        normed, unit_in, inv_in, latent_norm, unit_lat, inv_lat = [], [], [], [], [], []
        queries, keys, values, masks, cosines, sines = [], [], [], [], [], []
        for r in rows:
            x = layer_in[r].astype(F32)
            unit, inv = unit_norm(x)
            n1 = (unit * attn_gain).astype(BF)
            owners, inner = doc_layout(doc_lengths[r], places)
            key_owner, _ = doc_layout(doc_lengths[r], key_places)
            masks.append(
                (owners[:, None] == key_owner[None, :]) & (key_places[None, :] <= places[:, None])
            )
            angles = inner.astype(F32)[:, None] * frequency
            cosine, sine = jnp.cos(angles), jnp.sin(angles)
            kv = matmul(n1, key_value)
            k_own = turn(kv[:, :HD], cosine, sine).astype(BF)
            v_own = kv[:, HD:].astype(BF)
            order = list(range(1, seq_bits))
            keys.append(jnp.concatenate(seq_gather(k_own, order + [0]), axis=0))
            values.append(jnp.concatenate(seq_gather(v_own, order[::-1] + [0]), axis=0))
            lat = matmul(n1, query_down)
            ul, il = unit_norm(lat)
            ln = (ul * latent_gain).astype(BF)
            raw = matmul(ln, query_up).reshape(length, heads, HD)
            q = turn(raw, cosine[:, None, :], sine[:, None, :]).astype(BF)
            queries.append(q.transpose(1, 0, 2).reshape(heads * length, HD))
            normed.append(n1), unit_in.append(unit), inv_in.append(inv)
            latent_norm.append(ln), unit_lat.append(own(ul)), inv_lat.append(own(il))
            cosines.append(cosine), sines.append(sine)

        def masked(r, scores):
            shaped = scores.reshape(heads, length, -1)
            return shaped, masks[r][None]

        context, log_total, context_low = [], [], []
        middle, normed2, unit_mid, inv_mid = [], [], [], []
        for r in rows:
            scores, allowed = masked(r, dot_cols(queries[r], keys[r]) * scale)
            scores = jnp.where(allowed, scores, NEG_FILL)
            peak = jnp.max(scores, axis=-1, keepdims=True)
            expo = jnp.where(allowed, jnp.exp(scores - peak), 0.0)
            total = jnp.sum(expo, axis=-1, keepdims=True)
            ctx = matmul(expo.astype(BF).reshape(heads * length, -1), values[r])
            ctx = ctx.reshape(heads, length, HD) / total
            log_total.append(peak + jnp.log(total))
            context.append(ctx)
            flat = ctx.astype(BF).transpose(1, 0, 2).reshape(length, heads * HD)
            context_low.append(flat)
            attn = tp_scatter(matmul(flat, attn_out), tp_me)
            mid = own(layer_in[r]).astype(F32) + attn
            unit, inv = unit_norm(mid)
            middle.append(mid), unit_mid.append(unit), inv_mid.append(inv)
            normed2.append(tp_gather((unit * ffn_gain).astype(BF), tp_me))

        hidden, gate_delta, up_delta, layer_out = [], [], [], []
        mid_low, mid_delta, gain_mid = [], [], 0.0
        for r in rows:
            dhidden = dot_cols(out_grad[r], down_proj)
            gate = matmul(normed2[r], gate_proj)
            up = matmul(normed2[r], up_proj)
            sig = jax.nn.sigmoid(gate)
            swish = gate * sig
            hid = (swish * up).astype(BF)
            dgate = (dhidden * up * sig * (1.0 + gate * (1.0 - sig))).astype(BF)
            dup = (dhidden * swish).astype(BF)
            hidden.append(hid), gate_delta.append(dgate), up_delta.append(dup)
            d2 = tp_scatter(dot_cols(dgate, gate_proj) + dot_cols(dup, up_proj), tp_me)
            gain_mid = gain_mid + jnp.sum(d2 * unit_mid[r], axis=0)
            delta = own(out_grad[r]).astype(F32) + rms_backward(d2, unit_mid[r], inv_mid[r], ffn_gain)
            mid_low.append(tp_gather(delta.astype(BF), tp_me))
        for r in rows:
            ffn = tp_scatter(matmul(hidden[r], down_proj), tp_me)
            layer_out.append(tp_gather((middle[r] + ffn).astype(BF), tp_me))

        def joined(parts):
            return jnp.concatenate(parts, axis=0)

        dy_pair = split_cols(joined([out_grad[r] for r in rows]), me_bits)
        down_grad = grad_cols(joined(hidden), dy_pair, me_bits)
        n2_pair = split_cols(joined(normed2), me_bits)
        gate_grad = grad_rows(n2_pair, joined(gate_delta), me_bits)
        up_grad = grad_rows(n2_pair, joined(up_delta), me_bits)

        latent_delta, kv_delta, query_delta, gain_lat = [], [], [], 0.0
        for r in rows:
            dctx = dot_cols(mid_low[r], attn_out).astype(BF)
            dctx = dctx.reshape(length, heads, HD).transpose(1, 0, 2)
            row_delta = jnp.sum(dctx.astype(F32) * context[r], axis=-1, keepdims=True)
            dctx = dctx.reshape(heads * length, HD)
            scores, allowed = masked(r, dot_cols(queries[r], keys[r]) * scale)
            probs = jnp.where(allowed, jnp.exp(scores - log_total[r]), 0.0)
            dprobs = dot_cols(dctx, values[r]).reshape(probs.shape)
            dscores = (probs * (dprobs - row_delta)).astype(BF).reshape(heads * length, -1)
            dq = matmul(dscores, keys[r]) * scale
            dk = dot_rows(dscores, queries[r]) * scale
            dv = dot_rows(probs.astype(BF).reshape(heads * length, -1), dctx)
            dkv = jnp.concatenate([dk, dv], axis=-1).astype(BF).reshape(n_seq, length, 2 * HD)
            got = swap(dkv.reshape(n_seq // 2, 2, length, 2 * HD)[:, 1], "seq", 0)
            kept = dkv.reshape(n_seq // 2, 2, length, 2 * HD)[:, 0].astype(F32) + got.astype(F32)
            kept = kept.astype(BF).reshape([2] * len(upper) + [length, 2 * HD])
            zero_bits = [0] * seq_bits
            kv_sum = seq_finish(kept, zero_bits, upper)
            dq = dq.reshape(heads, length, HD).transpose(1, 0, 2)
            q_low = turn(dq, cosines[r][:, None, :], -sines[r][:, None, :]).astype(BF)
            q_low = q_low.reshape(length, heads * HD)
            query_delta.append(q_low)
            lat = tp_scatter(dot_cols(q_low, query_up), tp_me)
            gain_lat = gain_lat + jnp.sum(lat * unit_lat[r], axis=0)
            lat_low = rms_backward(lat, unit_lat[r], inv_lat[r], latent_gain).astype(BF)
            latent_delta.append(tp_gather(lat_low, tp_me))
            kv_own = tp_scatter(kv_sum, tp_me)
            dk_own = turn(kv_own[:, :HD], own(cosines[r]), -own(sines[r]))
            kv_low = jnp.concatenate([dk_own, kv_own[:, HD:]], axis=-1).astype(BF)
            kv_delta.append(tp_gather(kv_low, tp_me))

        low_pair = split_cols(joined(mid_low), me_bits)
        out_weight_grad = grad_cols(joined(context_low), low_pair, me_bits)
        lat_pair = split_cols(joined(latent_norm), me_bits)
        query_up_grad = grad_rows(lat_pair, joined(query_delta), me_bits)

        input_grad, gain_in = [], 0.0
        for r in rows:
            dn = dot_cols(latent_delta[r], query_down) + dot_cols(kv_delta[r], key_value)
            gain_in = gain_in + jnp.sum(dn * unit_in[r], axis=0)
            delta = mid_low[r].astype(F32) + rms_backward(dn, unit_in[r], inv_in[r], attn_gain)
            input_grad.append(delta.astype(BF))

        lat_cols = query_down.shape[1] // n_tp
        kv_cols = key_value.shape[1] // n_tp
        lat_all, kv_all = joined(latent_delta), joined(kv_delta)
        part = jnp.concatenate(
            [
                lax.dynamic_slice_in_dim(lat_all, tp_me * lat_cols, lat_cols, 1),
                lax.dynamic_slice_in_dim(kv_all, tp_me * kv_cols, kv_cols, 1),
            ],
            axis=1,
        )
        shared = grad_rows(split_cols(joined(normed), me_bits), part, me_bits)
        shared = tp_gather(shared.astype(BF), tp_me).reshape(n_tp, -1, lat_cols + kv_cols)
        shared = shared.astype(F32)
        down_q = shared[:, :, :lat_cols].transpose(1, 0, 2).reshape(-1, n_tp * lat_cols)
        kv_grad = shared[:, :, lat_cols:].transpose(1, 0, 2).reshape(-1, n_tp * kv_cols)

        gains = jnp.concatenate(
            [
                jnp.where(tp_me == 0, gain_in, 0.0).reshape(n_seq, -1),
                gain_mid.reshape(n_seq, -1),
                gain_lat.reshape(n_seq, -1),
            ],
            axis=1,
        )
        gains = gains.reshape([2] * seq_bits + [-1])
        left = list(reversed(range(seq_bits)))
        for bit in range(seq_bits):
            gains = halve(gains, me_bits, bit, left, True)
            left.remove(bit)
        for bit in range(tp_bits):
            gains = gains + swap(gains, "tp", bit)
        d_part = model_dim // n_seq
        return (
            jnp.stack(layer_out),
            jnp.stack(input_grad),
            gains[:d_part],
            down_q,
            gains[2 * d_part :],
            query_up_grad,
            kv_grad,
            out_weight_grad,
            gains[d_part : 2 * d_part],
            gate_grad,
            up_grad,
            down_grad,
        )

    return shards


def solution(mesh):
    return jax.shard_map(
        build(mesh.shape["seq"], mesh.shape["tp"]),
        mesh=mesh,
        in_specs=(
            P(None, "seq", None), P(), P(), P(), P(None, "tp"), P(), P("tp", None), P(),
            P(None, "tp"), P(None, "tp"), P("tp", None), P(None, "seq", None), P(),
        ),
        out_specs=(
            P(None, "seq", None), P(None, "seq", None), P("seq"), P("seq", None), P("seq"),
            P("seq", "tp"), P("seq", None), P("tp", "seq"), P("seq"), P("seq", "tp"),
            P("seq", "tp"), P("tp", "seq"),
        ),
        check_vma=False,
    )
```

time: 1370 us -> 927 us (0.68)
  waiting for transfers between devices: 1060 us -> 278 us
  local copies, waits for them, and re-layouts: 32.7 us -> 223 us
  starting transfers between devices: 0.96 us -> 125 us
  other arithmetic: 54.6 us -> 128 us
  blocking collectives: 24.2 us -> 0 us
  matrix products: 172 us -> 155 us
    psum x3 -> x0, waiting for transfers between devices: 526 us -> none  [the longest x1 218 us: shards(): ffn_total = lax.psum(matmul(hidden, down_proj), 'tp')]
    reduce_scatter x8 -> x0, waiting for transfers between devices: 515 us -> none  [the longest x1 91.3 us: shards(): lax.psum_scatter(upproj_grad, 'seq', scatter_dimension=0, tiled=True)]
    ppermute x0 -> x99, waiting for transfers between devices: none -> 278 us  [swap(): return lax.ppermute(value, axis, [(i, i ^ 1 << bit) for i in range(count)])]
    ppermute x0 -> x99, starting transfers between devices: none -> 125 us  [swap(): return lax.ppermute(value, axis, [(i, i ^ 1 << bit) for i in range(count)])]
    dot_general x13 -> x18, matrix products: 91.1 us -> 44.2 us  [matmul(): return jnp.dot(left, right, preferred_element_type=F32)]
    dynamic_slice x0 -> x14, local copies, waits for them, and re-layouts: none -> 43.7 us  [pick(): return lax.dynamic_index_in_dim(blocks, where, axis, keepdims=False)]
    unnamed x137 -> x450, local copies, waits for them, and re-layouts: 20.8 us -> 62.4 us
    dot_general x7 -> x18, matrix products: 32.6 us -> 66.4 us  [dot_cols(): lax.dot_general(left, right, (((1,), (1,)), ((), ())), preferred_element_...]
  transfers between devices with their start and end apart: 12 -> 99, of which waited for: 11 -> 51; matrix products, arithmetic and copies ran while one was open for 8% -> 50% of each run, Pallas kernels for 0% -> 0%
where the time goes in v1:
time: 927 us; the launch traced here: 914 us
  waiting for transfers between devices  278 us (30%)
  local copies, waits for them, and re-layouts  223 us (24%)
  matrix products  155 us (17%)
  other arithmetic  128 us (14%)
  starting transfers between devices  125 us (13%)
    ppermute x99, waiting for transfers between devices, swap(): return lax.ppermute(value, axis, [(i, i ^ 1 << bit) for i in range(count)])  278 us
    ppermute x99, starting transfers between devices, swap(): return lax.ppermute(value, axis, [(i, i ^ 1 << bit) for i in range(count)])  125 us
    dot_general x18, matrix products, dot_cols(): lax.dot_general(left, right, (((1,), (1,)), ((), ())), preferred_element_...  66.4 us
    unnamed x450, local copies, waits for them, and re-layouts  62.4 us
    dot_general x16, matrix products, dot_rows(): lax.dot_general(left, right, (((0,), (0,)), ((), ())), preferred_element_...  44.8 us
    dot_general x18, matrix products, matmul(): return jnp.dot(left, right, preferred_element_type=F32)  44.2 us
    dynamic_slice x14, local copies, waits for them, and re-layouts, pick(): return lax.dynamic_index_in_dim(blocks, where, axis, keepdims=False)  43.7 us
    concatenate x10, local copies, waits for them, and re-layouts, joined(): return jnp.concatenate(parts, axis=0)  19.8 us
  transfers between devices with their start and end apart: 99, of which 51 were waited for; matrix products, arithmetic and copies ran while one was open for 50% of the time, Pallas kernels for 0%

profile of v1, /device:TPU:0, one launch (start us, length us, event | category | flops | bytes accessed | tf_op | source)
XLA Modules:
  0.0 913.9 jit_solution(13784737076566320183)
XLA Ops:
  128.6 4.9 fusion.4
  142.7 4.9 fusion.64
  157.9 4.6 fusion.6
  171.7 4.9 fusion.60
  186.8 5.7 fusion.9
  192.5 6.8 collective-permute-done.7
  205.8 17.1 %collective-permute-done.8 = bf16[1,64,2048]{2,1,0:T(8,128)(2,1)S(1)} collective-permute-done((bf16[1,64,2048]{2,1,0:T(8,128)(2,1)S(1)}, bf16[1,64,2048]{2,1,0:T(8,128)(2,1)S(1)}, u32[]{:S(2)}, u32[]{:S(2)}) %collective-permute-start.8) | collective-permute-done | bytes 262176 | tf_op jit(solution)/shard_map/ppermute | solution.py:57
  228.6 9.8 %collective-permute-done.9 = bf16[2,64,2048]{2,1,0:T(8,128)(2,1)S(1)} collective-permute-done((bf16[2,64,2048]{2,1,0:T(8,128)(2,1)S(1)}, bf16[2,64,2048]{2,1,0:T(8,128)(2,1)S(1)}, u32[]{:S(2)}, u32[]{:S(2)}) %collective-permute-start.9) | collective-permute-done | bytes 524320 | tf_op jit(solution)/shard_map/ppermute | solution.py:57
  254.9 10.8 %collective-permute-done.28 = bf16[2,64,2048]{2,1,0:T(8,128)(2,1)S(1)} collective-permute-done((bf16[2,64,2048]{2,1,0:T(8,128)(2,1)S(1)}, bf16[2,64,2048]{2,1,0:T(8,128)(2,1)S(1)}, u32[]{:S(2)}, u32[]{:S(2)}) %collective-permute-start.28) | collective-permute-done | bytes 524320 | tf_op jit(solution)/shard_map/ppermute | solution.py:57
  268.0 13.6 %collective-permute-done.10 = bf16[2,64,2048]{2,1,0:T(8,128)(2,1)S(1)} collective-permute-done((bf16[2,64,2048]{2,1,0:T(8,128)(2,1)S(1)}, bf16[2,64,2048]{2,1,0:T(8,128)(2,1)S(1)}, u32[]{:S(2)}, u32[]{:S(2)}) %collective-permute-start.10) | collective-permute-done | bytes 524320 | tf_op jit(solution)/shard_map/ppermute | solution.py:57
  283.8 12.0 %collective-permute-done.11 = bf16[1,64,2048]{2,1,0:T(8,128)(2,1)S(1)} collective-permute-done((bf16[1,64,2048]{2,1,0:T(8,128)(2,1)S(1)}, bf16[1,64,2048]{2,1,0:T(8,128)(2,1)S(1)}, u32[]{:S(2)}, u32[]{:S(2)}) %collective-permute-start.11) | collective-permute-done | bytes 262176 | tf_op jit(solution)/shard_map/ppermute | solution.py:57
  301.0 7.9 dot_general.206
  308.8 7.9 dot_general.219
  328.5 14.3 %collective-permute-done.30 = bf16[1,64,2048]{2,1,0:T(8,128)(2,1)S(1)} collective-permute-done((bf16[1,64,2048]{2,1,0:T(8,128)(2,1)S(1)}, bf16[1,64,2048]{2,1,0:T(8,128)(2,1)S(1)}, u32[]{:S(2)}, u32[]{:S(2)}) %collective-permute-start.30) | collective-permute-done | bytes 262176 | tf_op jit(solution)/shard_map/ppermute | solution.py:57
  349.3 6.0 fusion.198
  360.4 7.1 multiply_convert_fusion.6
  367.5 5.8 convolution_convert_fusion.5
  377.5 6.3 constant_dynamic-slice_fusion.1
  383.8 5.0 copy.261
  388.9 6.1 fusion.202
  402.3 5.8 copy.260
  409.1 6.3 fusion.17
  427.6 7.4 multiply_convert_fusion.1
  455.1 7.1 collective-permute-done.45
  468.3 5.8 collective-permute-done.46
  477.5 7.3 collective-permute-done.25
  488.4 10.5 %collective-permute-done.47 = bf16[1,64,2048]{2,1,0:T(8,128)(2,1)} collective-permute-done((bf16[1,64,2048]{2,1,0:T(8,128)(2,1)}, bf16[1,64,2048]{2,1,0:T(8,128)(2,1)}, u32[]{:S(2)}, u32[]{:S(2)}) %collective-permute-start.47) | collective-permute-done | bytes 262176 | tf_op jit(solution)/shard_map/ppermute | solution.py:57
  501.0 16.7 %collective-permute-start.48 = (bf16[2,64,2048]{2,1,0:T(8,128)(2,1)}, bf16[2,64,2048]{2,1,0:T(8,128)(2,1)}, u32[]{:S(2)}, u32[]{:S(2)}) collective-permute-start(bf16[2,64,2048]{2,1,0:T(8,128)(2,1)} %maximum_bitcast_fusion.5), channel_id=1, source_target_pairs={{0,1},{1,0},{2,3},{3,2},{4,5},{5,4},{6,7},{7,6},{8,9},{9,8},{10,11... | collective-permute-start | bytes 1572872 | tf_op jit(solution)/shard_map/ppermute | solution.py:57
  530.5 6.2 collective-permute-done.39
  537.1 4.6 collective-permute-done.38
  556.4 8.6 constant_dynamic-slice_fusion.3
  565.0 6.2 copy.255
  571.2 5.8 copy.254
  584.2 6.1 multiply_convert_fusion
  644.4 6.6 collective-permute-done.34
  651.1 6.9 collective-permute-done.51
  658.3 6.5 collective-permute-done.35
  666.2 5.0 collective-permute-done.52
  687.3 6.0 add_convert_fusion
  693.3 4.8 copy.265
  722.8 16.9 %collective-permute-done.55 = bf16[128,512]{1,0:T(8,128)(2,1)S(1)} collective-permute-done((bf16[128,512]{1,0:T(8,128)(2,1)S(1)}, bf16[128,512]{1,0:T(8,128)(2,1)S(1)}, u32[]{:S(2)}, u32[]{:S(2)}) %collective-permute-start.55) | collective-permute-done | bytes 131104 | tf_op jit(solution)/shard_map/ppermute | solution.py:57
  740.0 4.8 collective-permute-done.57
  811.4 9.3 %collective-permute-done.92 = bf16[2,128,1408]{2,1,0:T(8,128)(2,1)S(1)} collective-permute-done((bf16[2,128,1408]{2,1,0:T(8,128)(2,1)S(1)}, bf16[2,128,1408]{2,1,0:T(8,128)(2,1)S(1)}, u32[]{:S(2)}, u32[]{:S(2)}) %collective-permute-start.92) | collective-permute-done | bytes 720928 | tf_op jit(solution)/shard_map/ppermute | solution.py:57
  825.1 11.1 %collective-permute-done.87 = bf16[2,128,1408]{2,1,0:T(8,128)(2,1)S(1)} collective-permute-done((bf16[2,128,1408]{2,1,0:T(8,128)(2,1)S(1)}, bf16[2,128,1408]{2,1,0:T(8,128)(2,1)S(1)}, u32[]{:S(2)}, u32[]{:S(2)}) %collective-permute-start.87) | collective-permute-done | bytes 720928 | tf_op jit(solution)/shard_map/ppermute | solution.py:57
  855.1 5.5 collective-permute-done.86
  885.8 4.8 collective-permute-done.71
  893.0 6.1 collective-permute-done.72
  901.7 5.4 collective-permute-done.73
  (987 shorter events, 543.5 us)
Async XLA Ops:
  11.5 95.0 %collective-permute-start = (bf16[1,256,256]{2,1,0:T(8,128)(2,1)}, bf16[1,256,256]{2,1,0:T(8,128)(2,1)}, u32[]{:S(2)}, u32[]{:S(2)}) collective-permute-start(bf16[1,256,256]{2,1,0:T(8,128)(2,1)} %pad_maximum_fusion.66), channel_id=1, source_target_pairs={{0,8},{4,12},{8,0},{12,4},{16,24},{20,28},{24,16},{28,20},{1,9},{5... | collective-permute-start | bytes 393224 | tf_op jit(solution)/shard_map/ppermute | solution.py:57
  15.2 94.3 %collective-permute-start.3 = (bf16[1,256,256]{2,1,0:T(8,128)(2,1)}, bf16[1,256,256]{2,1,0:T(8,128)(2,1)}, u32[]{:S(2)}, u32[]{:S(2)}) collective-permute-start(bf16[1,256,256]{2,1,0:T(8,128)(2,1)} %get-tuple-element.160), channel_id=1, source_target_pairs={{0,16},{4,20},{8,24},{12,28},{16,0},{20,4},{24,8},{28,12},{1,17},{... | collective-permute-start | bytes 393224 | tf_op jit(solution)/shard_map/ppermute | solution.py:57
  17.4 94.7 %collective-permute-start.14 = (bf16[1,256,256]{2,1,0:T(8,128)(2,1)}, bf16[1,256,256]{2,1,0:T(8,128)(2,1)}, u32[]{:S(2)}, u32[]{:S(2)}) collective-permute-start(bf16[1,256,256]{2,1,0:T(8,128)(2,1)} %pad_maximum_fusion.67), channel_id=1, source_target_pairs={{0,8},{4,12},{8,0},{12,4},{16,24},{20,28},{24,16},{28,20},{1,9},{5... | collective-permute-start | bytes 393224 | tf_op jit(solution)/shard_map/ppermute | solution.py:57
  18.6 95.0 %collective-permute-start.17 = (bf16[1,256,256]{2,1,0:T(8,128)(2,1)}, bf16[1,256,256]{2,1,0:T(8,128)(2,1)}, u32[]{:S(2)}, u32[]{:S(2)}) collective-permute-start(bf16[1,256,256]{2,1,0:T(8,128)(2,1)} %get-tuple-element.166), channel_id=1, source_target_pairs={{0,16},{4,20},{8,24},{12,28},{16,0},{20,4},{24,8},{28,12},{1,17},{... | collective-permute-start | bytes 393224 | tf_op jit(solution)/shard_map/ppermute | solution.py:57
  123.2 28.2 %collective-permute-start.16 = (bf16[4,256,256]{2,1,0:T(8,128)(2,1)}, bf16[4,256,256]{2,1,0:T(8,128)(2,1)}, u32[]{:S(2)}, u32[]{:S(2)}) collective-permute-start(bf16[4,256,256]{2,1,0:T(8,128)(2,1)} %pad_maximum_fusion.45), channel_id=1, source_target_pairs={{0,4},{4,0},{8,12},{12,8},{16,20},{20,16},{24,28},{28,24},{1,5},{5... | collective-permute-start | bytes 1572872 | tf_op jit(solution)/shard_map/ppermute | solution.py:57
  125.6 36.9 %collective-permute-start.19 = (bf16[4,256,256]{2,1,0:T(8,128)(2,1)}, bf16[4,256,256]{2,1,0:T(8,128)(2,1)}, u32[]{:S(2)}, u32[]{:S(2)}) collective-permute-start(bf16[4,256,256]{2,1,0:T(8,128)(2,1)} %pad_maximum_fusion.46), channel_id=1, source_target_pairs={{0,4},{4,0},{8,12},{12,8},{16,20},{20,16},{24,28},{28,24},{1,5},{5... | collective-permute-start | bytes 1572872 | tf_op jit(solution)/shard_map/ppermute | solution.py:57
  149.8 32.2 %collective-permute-start.6 = (bf16[2,64,2048]{2,1,0:T(8,128)(2,1)}, bf16[2,64,2048]{2,1,0:T(8,128)(2,1)}, u32[]{:S(2)}, u32[]{:S(2)}) collective-permute-start(bf16[2,64,2048]{2,1,0:T(8,128)(2,1)} %dynamic-slice_bitcast_fusion.13), channel_id=1, source_target_pairs={{0,1},{1,0},{2,3},{3,2},{4,5},{5,4},{6,7},{7,6},{8,9},{9,8},{10,11... | collective-permute-start | bytes 1572872 | tf_op jit(solution)/shard_map/ppermute | solution.py:57
  181.5 23.0 %collective-permute-start.20 = (bf16[2,64,2048]{2,1,0:T(8,128)(2,1)}, bf16[2,64,2048]{2,1,0:T(8,128)(2,1)}, u32[]{:S(2)}, u32[]{:S(2)}) collective-permute-start(bf16[2,64,2048]{2,1,0:T(8,128)(2,1)} %dynamic-slice_bitcast_fusion.11), channel_id=1, source_target_pairs={{0,1},{1,0},{2,3},{3,2},{4,5},{5,4},{6,7},{7,6},{8,9},{9,8},{10,11... | collective-permute-start | bytes 1572872 | tf_op jit(solution)/shard_map/ppermute | solution.py:57
  184.2 15.2 %collective-permute-start.7 = (bf16[1,64,2048]{2,1,0:T(8,128)(2,1)S(1)}, bf16[1,64,2048]{2,1,0:T(8,128)(2,1)}, u32[]{:S(2)}, u32[]{:S(2)}) collective-permute-start(bf16[1,64,2048]{2,1,0:T(8,128)(2,1)S(1)} %constant_dynamic-slice_fusion.23), channel_id=1, source_target_pairs={{0,2},{1,3},{2,0},{3,1},{4,6},{5,7},{6,4},{7,5},{8,10},{9,11},{10,... | collective-permute-start | bytes 786440 | tf_op jit(solution)/shard_map/ppermute | solution.py:57
  201.0 22.0 %collective-permute-start.8 = (bf16[1,64,2048]{2,1,0:T(8,128)(2,1)S(1)}, bf16[1,64,2048]{2,1,0:T(8,128)(2,1)S(1)}, u32[]{:S(2)}, u32[]{:S(2)}) collective-permute-start(bf16[1,64,2048]{2,1,0:T(8,128)(2,1)S(1)} %multiply_convert_fusion.15), channel_id=1, source_target_pairs={{0,2},{1,3},{2,0},{3,1},{4,6},{5,7},{6,4},{7,5},{8,10},{9,11},{10,... | collective-permute-start | bytes 786440 | tf_op jit(solution)/shard_map/ppermute | solution.py:57
  205.7 21.6 %collective-permute-start.21 = (bf16[1,64,2048]{2,1,0:T(8,128)(2,1)S(1)}, bf16[1,64,2048]{2,1,0:T(8,128)(2,1)S(1)}, u32[]{:S(2)}, u32[]{:S(2)}) collective-permute-start(bf16[1,64,2048]{2,1,0:T(8,128)(2,1)S(1)} %constant_dynamic-slice_fusion.21), channel_id=1, source_target_pairs={{0,2},{1,3},{2,0},{3,1},{4,6},{5,7},{6,4},{7,5},{8,10},{9,11},{10,... | collective-permute-start | bytes 786440 | tf_op jit(solution)/shard_map/ppermute | solution.py:57
  223.2 15.2 %collective-permute-start.9 = (bf16[2,64,2048]{2,1,0:T(8,128)(2,1)S(1)}, bf16[2,64,2048]{2,1,0:T(8,128)(2,1)S(1)}, u32[]{:S(2)}, u32[]{:S(2)}) collective-permute-start(bf16[2,64,2048]{2,1,0:T(8,128)(2,1)S(1)} %maximum_bitcast_fusion), channel_id=1, source_target_pairs={{0,1},{1,0},{2,3},{3,2},{4,5},{5,4},{6,7},{7,6},{8,9},{9,8},{10,11... | collective-permute-start | bytes 1572872 | tf_op jit(solution)/shard_map/ppermute | solution.py:57
  252.8 28.8 %collective-permute-start.10 = (bf16[2,64,2048]{2,1,0:T(8,128)(2,1)S(1)}, bf16[2,64,2048]{2,1,0:T(8,128)(2,1)S(1)}, u32[]{:S(2)}, u32[]{:S(2)}) collective-permute-start(bf16[2,64,2048]{2,1,0:T(8,128)(2,1)S(1)} %dynamic-slice_bitcast_fusion.12), channel_id=1, source_target_pairs={{0,1},{1,0},{2,3},{3,2},{4,5},{5,4},{6,7},{7,6},{8,9},{9,8},{10,11... | collective-permute-start | bytes 1572872 | tf_op jit(solution)/shard_map/ppermute | solution.py:57
  265.9 17.6 %collective-permute-start.29 = (bf16[1,64,2048]{2,1,0:T(8,128)(2,1)S(1)}, bf16[1,64,2048]{2,1,0:T(8,128)(2,1)S(1)}, u32[]{:S(2)}, u32[]{:S(2)}) collective-permute-start(bf16[1,64,2048]{2,1,0:T(8,128)(2,1)S(1)} %constant_dynamic-slice_fusion.19), channel_id=1, source_target_pairs={{0,2},{1,3},{2,0},{3,1},{4,6},{5,7},{6,4},{7,5},{8,10},{9,11},{10,... | collective-permute-start | bytes 786440 | tf_op jit(solution)/shard_map/ppermute | solution.py:57
  297.9 26.4 %collective-permute-start.22 = (bf16[1,64,2048]{2,1,0:T(8,128)(2,1)}, bf16[1,64,2048]{2,1,0:T(8,128)(2,1)}, u32[]{:S(2)}, u32[]{:S(2)}) collective-permute-start(bf16[1,64,2048]{2,1,0:T(8,128)(2,1)} %get-tuple-element.198), channel_id=1, source_target_pairs={{0,2},{1,3},{2,0},{3,1},{4,6},{5,7},{6,4},{7,5},{8,10},{9,11},{10,... | collective-permute-start | bytes 786440 | tf_op jit(solution)/shard_map/ppermute | solution.py:57
  321.3 21.5 %collective-permute-start.30 = (bf16[1,64,2048]{2,1,0:T(8,128)(2,1)S(1)}, bf16[1,64,2048]{2,1,0:T(8,128)(2,1)S(1)}, u32[]{:S(2)}, u32[]{:S(2)}) collective-permute-start(bf16[1,64,2048]{2,1,0:T(8,128)(2,1)S(1)} %copy-done.116), channel_id=1, source_target_pairs={{0,2},{1,3},{2,0},{3,1},{4,6},{5,7},{6,4},{7,5},{8,10},{9,11},{10,... | collective-permute-start | bytes 786440 | tf_op jit(solution)/shard_map/ppermute | solution.py:57
  324.2 22.2 %collective-permute-start.12 = (bf16[1,64,2048]{2,1,0:T(8,128)(2,1)S(1)}, bf16[1,64,2048]{2,1,0:T(8,128)(2,1)S(1)}, u32[]{:S(2)}, u32[]{:S(2)}) collective-permute-start(bf16[1,64,2048]{2,1,0:T(8,128)(2,1)S(1)} %get-tuple-element.149), channel_id=1, source_target_pairs={{0,2},{1,3},{2,0},{3,1},{4,6},{5,7},{6,4},{7,5},{8,10},{9,11},{10,... | collective-permute-start | bytes 786440 | tf_op jit(solution)/shard_map/ppermute | solution.py:57
  325.4 23.6 %collective-permute-start.23 = (bf16[2,64,2048]{2,1,0:T(8,128)(2,1)S(1)}, bf16[2,64,2048]{2,1,0:T(8,128)(2,1)S(1)}, u32[]{:S(2)}, u32[]{:S(2)}) collective-permute-start(bf16[2,64,2048]{2,1,0:T(8,128)(2,1)S(1)} %maximum_bitcast_fusion.2), channel_id=1, source_target_pairs={{0,1},{1,0},{2,3},{3,2},{4,5},{5,4},{6,7},{7,6},{8,9},{9,8},{10,11... | collective-permute-start | bytes 1572872 | tf_op jit(solution)/shard_map/ppermute | solution.py:57
  343.8 71.6 %collective-permute-start.31 = (bf16[2,64,2048]{2,1,0:T(8,128)(2,1)}, bf16[2,64,2048]{2,1,0:T(8,128)(2,1)}, u32[]{:S(2)}, u32[]{:S(2)}) collective-permute-start(bf16[2,64,2048]{2,1,0:T(8,128)(2,1)} %maximum_bitcast_fusion.4), channel_id=1, source_target_pairs={{0,1},{1,0},{2,3},{3,2},{4,5},{5,4},{6,7},{7,6},{8,9},{9,8},{10,11... | collective-permute-start | bytes 1572872 | tf_op jit(solution)/shard_map/ppermute | solution.py:57
  348.1 100.1 %collective-permute-start.13 = (bf16[2,64,2048]{2,1,0:T(8,128)(2,1)}, bf16[2,64,2048]{2,1,0:T(8,128)(2,1)}, u32[]{:S(2)}, u32[]{:S(2)}) collective-permute-start(bf16[2,64,2048]{2,1,0:T(8,128)(2,1)} %maximum_bitcast_fusion.1), channel_id=1, source_target_pairs={{0,1},{1,0},{2,3},{3,2},{4,5},{5,4},{6,7},{7,6},{8,9},{9,8},{10,11... | collective-permute-start | bytes 1572872 | tf_op jit(solution)/shard_map/ppermute | solution.py:57
  376.7 310.6 %collective-permute-start.94 = (bf16[1408,1024]{0,1:T(8,128)(2,1)}, bf16[1408,1024]{0,1:T(8,128)(2,1)}, u32[]{:S(2)}, u32[]{:S(2)}) collective-permute-start(bf16[1408,1024]{0,1:T(8,128)(2,1)} %convolution_convert_fusion), channel_id=1, source_target_pairs={{0,4},{4,0},{8,12},{12,8},{16,20},{20,16},{24,28},{28,24},{1,5},{5... | collective-permute-start | bytes 8650760 | tf_op jit(solution)/shard_map/ppermute | solution.py:57
  401.8 296.4 %collective-permute-start.89 = (bf16[1024,1408]{1,0:T(8,128)(2,1)}, bf16[1024,1408]{1,0:T(8,128)(2,1)}, u32[]{:S(2)}, u32[]{:S(2)}) collective-permute-start(bf16[1024,1408]{1,0:T(8,128)(2,1)} %convolution_convert_fusion.1), channel_id=1, source_target_pairs={{0,4},{4,0},{8,12},{12,8},{16,20},{20,16},{24,28},{28,24},{1,5},{5... | collective-permute-start | bytes 8650760 | tf_op jit(solution)/shard_map/ppermute | solution.py:57
  408.1 298.1 %collective-permute-start.84 = (bf16[1024,1408]{1,0:T(8,128)(2,1)}, bf16[1024,1408]{1,0:T(8,128)(2,1)}, u32[]{:S(2)}, u32[]{:S(2)}) collective-permute-start(bf16[1024,1408]{1,0:T(8,128)(2,1)} %convolution_convert_fusion.2), channel_id=1, source_target_pairs={{0,4},{4,0},{8,12},{12,8},{16,20},{20,16},{24,28},{28,24},{1,5},{5... | collective-permute-start | bytes 8650760 | tf_op jit(solution)/shard_map/ppermute | solution.py:57
  415.4 47.8 %collective-permute-start.24 = (bf16[2,64,2048]{2,1,0:T(8,128)(2,1)}, bf16[2,64,2048]{2,1,0:T(8,128)(2,1)}, u32[]{:S(2)}, u32[]{:S(2)}) collective-permute-start(bf16[2,64,2048]{2,1,0:T(8,128)(2,1)} %dynamic-slice_bitcast_fusion.10), channel_id=1, source_target_pairs={{0,1},{1,0},{2,3},{3,2},{4,5},{5,4},{6,7},{7,6},{8,9},{9,8},{10,11... | collective-permute-start | bytes 1572872 | tf_op jit(solution)/shard_map/ppermute | solution.py:57
  462.3 24.4 %collective-permute-start.32 = (bf16[2,64,1024]{2,1,0:T(8,128)(2,1)S(1)}, bf16[2,64,1024]{2,1,0:T(8,128)(2,1)S(1)}, u32[]{:S(2)}, u32[]{:S(2)}) collective-permute-start(bf16[2,64,1024]{2,1,0:T(8,128)(2,1)S(1)} %dynamic-slice_bitcast_fusion.25), channel_id=1, source_target_pairs={{0,1},{1,0},{2,3},{3,2},{4,5},{5,4},{6,7},{7,6},{8,9},{9,8},{10,11... | collective-permute-start | bytes 786440 | tf_op jit(solution)/shard_map/ppermute | solution.py:57
  484.8 16.2 %collective-permute-start.36 = (bf16[4,256,512]{1,2,0:T(8,128)(2,1)}, bf16[4,256,512]{1,2,0:T(8,128)(2,1)}, u32[]{:S(2)}, u32[]{:S(2)}) collective-permute-start(bf16[4,256,512]{1,2,0:T(8,128)(2,1)} %fusion.47), channel_id=1, source_target_pairs={{0,4},{4,0},{8,12},{12,8},{16,20},{20,16},{24,28},{28,24},{1,5},{5... | collective-permute-start | bytes 3145736 | tf_op jit(solution)/shard_map/ppermute | solution.py:57
  498.9 22.2 %collective-permute-start.26 = (bf16[1,64,2048]{2,1,0:T(8,128)(2,1)S(1)}, bf16[1,64,2048]{2,1,0:T(8,128)(2,1)}, u32[]{:S(2)}, u32[]{:S(2)}) collective-permute-start(bf16[1,64,2048]{2,1,0:T(8,128)(2,1)S(1)} %get-tuple-element.155), channel_id=1, source_target_pairs={{0,2},{1,3},{2,0},{3,1},{4,6},{5,7},{6,4},{7,5},{8,10},{9,11},{10,... | collective-permute-start | bytes 786440 | tf_op jit(solution)/shard_map/ppermute | solution.py:57
  501.0 47.0 %collective-permute-start.48 = (bf16[2,64,2048]{2,1,0:T(8,128)(2,1)}, bf16[2,64,2048]{2,1,0:T(8,128)(2,1)}, u32[]{:S(2)}, u32[]{:S(2)}) collective-permute-start(bf16[2,64,2048]{2,1,0:T(8,128)(2,1)} %maximum_bitcast_fusion.5), channel_id=1, source_target_pairs={{0,1},{1,0},{2,3},{3,2},{4,5},{5,4},{6,7},{7,6},{8,9},{9,8},{10,11... | collective-permute-start | bytes 1572872 | tf_op jit(solution)/shard_map/ppermute | solution.py:57
  546.6 84.2 %collective-permute-start.33 = (bf16[1,64,1024]{2,1,0:T(8,128)(2,1)}, bf16[1,64,1024]{2,1,0:T(8,128)(2,1)}, u32[]{:S(2)}, u32[]{:S(2)}) collective-permute-start(bf16[1,64,1024]{2,1,0:T(8,128)(2,1)} %constant_dynamic-slice_fusion.18), channel_id=1, source_target_pairs={{0,2},{1,3},{2,0},{3,1},{4,6},{5,7},{6,4},{7,5},{8,10},{9,11},{10,... | collective-permute-start | bytes 393224 | tf_op jit(solution)/shard_map/ppermute | solution.py:57
  548.0 56.5 %collective-permute-start.27 = (bf16[2,64,2048]{2,1,0:T(8,128)(2,1)}, bf16[2,64,2048]{2,1,0:T(8,128)(2,1)}, u32[]{:S(2)}, u32[]{:S(2)}) collective-permute-start(bf16[2,64,2048]{2,1,0:T(8,128)(2,1)} %maximum_bitcast_fusion.3), channel_id=1, source_target_pairs={{0,1},{1,0},{2,3},{3,2},{4,5},{5,4},{6,7},{7,6},{8,9},{9,8},{10,11... | collective-permute-start | bytes 1572872 | tf_op jit(solution)/shard_map/ppermute | solution.py:57
  630.9 46.5 %collective-permute-start.74 = (bf16[512,1024]{1,0:T(8,128)(2,1)S(1)}, bf16[512,1024]{1,0:T(8,128)(2,1)S(1)}, u32[]{:S(2)}, u32[]{:S(2)}) collective-permute-start(bf16[512,1024]{1,0:T(8,128)(2,1)S(1)} %convolution_convert_fusion.8), channel_id=1, source_target_pairs={{0,4},{4,0},{8,12},{12,8},{16,20},{20,16},{24,28},{28,24},{1,5},{5... | collective-permute-start | bytes 3145736 | tf_op jit(solution)/shard_map/ppermute | solution.py:57
  677.4 162.4 %collective-permute-start.79 = (bf16[1024,1024]{0,1:T(8,128)(2,1)}, bf16[1024,1024]{0,1:T(8,128)(2,1)}, u32[]{:S(2)}, u32[]{:S(2)}) collective-permute-start(bf16[1024,1024]{0,1:T(8,128)(2,1)} %convolution_convert_fusion.7), channel_id=1, source_target_pairs={{0,4},{4,0},{8,12},{12,8},{16,20},{20,16},{24,28},{28,24},{1,5},{5... | collective-permute-start | bytes 6291464 | tf_op jit(solution)/shard_map/ppermute | solution.py:57
  680.4 34.6 %collective-permute-start.75 = (bf16[2,64,1024]{2,1,0:T(8,128)(2,1)}, bf16[2,64,1024]{2,1,0:T(8,128)(2,1)}, u32[]{:S(2)}, u32[]{:S(2)}) collective-permute-start(bf16[2,64,1024]{2,1,0:T(8,128)(2,1)} %dynamic-slice_bitcast_fusion.23), channel_id=1, source_target_pairs={{0,8},{4,12},{8,0},{12,4},{16,24},{20,28},{24,16},{28,20},{1,9},{5... | collective-permute-start | bytes 786440 | tf_op jit(solution)/shard_map/ppermute | solution.py:57
  687.3 57.9 %collective-permute-start.77 = (bf16[2,64,1024]{2,1,0:T(8,128)(2,1)}, bf16[2,64,1024]{2,1,0:T(8,128)(2,1)}, u32[]{:S(2)}, u32[]{:S(2)}) collective-permute-start(bf16[2,64,1024]{2,1,0:T(8,128)(2,1)} %dynamic-slice_bitcast_fusion.22), channel_id=1, source_target_pairs={{0,16},{4,20},{8,24},{12,28},{16,0},{20,4},{24,8},{28,12},{1,17},{... | collective-permute-start | bytes 786440 | tf_op jit(solution)/shard_map/ppermute | solution.py:57
  698.1 21.5 %collective-permute-start.54 = (bf16[2,128,512]{2,1,0:T(8,128)(2,1)S(1)}, bf16[2,128,512]{2,1,0:T(8,128)(2,1)S(1)}, u32[]{:S(2)}, u32[]{:S(2)}) collective-permute-start(bf16[2,128,512]{2,1,0:T(8,128)(2,1)S(1)} %bitcast.1033), channel_id=1, source_target_pairs={{0,8},{4,12},{8,0},{12,4},{16,24},{20,28},{24,16},{28,20},{1,9},{5... | collective-permute-start | bytes 786440 | tf_op jit(solution)/shard_map/ppermute | solution.py:57
  707.0 15.5 %collective-permute-start.56 = (bf16[2,128,512]{2,1,0:T(8,128)(2,1)S(1)}, bf16[2,128,512]{2,1,0:T(8,128)(2,1)S(1)}, u32[]{:S(2)}, u32[]{:S(2)}) collective-permute-start(bf16[2,128,512]{2,1,0:T(8,128)(2,1)S(1)} %bitcast.1032), channel_id=1, source_target_pairs={{0,16},{4,20},{8,24},{12,28},{16,0},{20,4},{24,8},{28,12},{1,17},{... | collective-permute-start | bytes 786440 | tf_op jit(solution)/shard_map/ppermute | solution.py:57
  715.0 89.5 %collective-permute-start.95 = (bf16[2,704,256]{2,1,0:T(8,128)(2,1)}, bf16[2,704,256]{2,1,0:T(8,128)(2,1)}, u32[]{:S(2)}, u32[]{:S(2)}) collective-permute-start(bf16[2,704,256]{2,1,0:T(8,128)(2,1)} %dynamic-slice_bitcast_fusion.1), channel_id=1, source_target_pairs={{0,8},{4,12},{8,0},{12,4},{16,24},{20,28},{24,16},{28,20},{1,9},{5... | collective-permute-start | bytes 2162696 | tf_op jit(solution)/shard_map/ppermute | solution.py:57
  719.6 87.3 %collective-permute-start.97 = (bf16[2,704,256]{2,1,0:T(8,128)(2,1)}, bf16[2,704,256]{2,1,0:T(8,128)(2,1)}, u32[]{:S(2)}, u32[]{:S(2)}) collective-permute-start(bf16[2,704,256]{2,1,0:T(8,128)(2,1)} %dynamic-slice_bitcast_fusion), channel_id=1, source_target_pairs={{0,16},{4,20},{8,24},{12,28},{16,0},{20,4},{24,8},{28,12},{1,17},{... | collective-permute-start | bytes 2162696 | tf_op jit(solution)/shard_map/ppermute | solution.py:57
  722.5 17.2 %collective-permute-start.55 = (bf16[128,512]{1,0:T(8,128)(2,1)S(1)}, bf16[128,512]{1,0:T(8,128)(2,1)S(1)}, u32[]{:S(2)}, u32[]{:S(2)}) collective-permute-start(bf16[128,512]{1,0:T(8,128)(2,1)S(1)} %slice_bitcast_fusion.4), channel_id=1, source_target_pairs={{0,16},{4,20},{8,24},{12,28},{16,0},{20,4},{24,8},{28,12},{1,17},{... | collective-permute-start | bytes 393224 | tf_op jit(solution)/shard_map/ppermute | solution.py:57
  744.8 64.5 %collective-permute-start.90 = (bf16[2,128,1408]{2,1,0:T(8,128)(2,1)}, bf16[2,128,1408]{2,1,0:T(8,128)(2,1)}, u32[]{:S(2)}, u32[]{:S(2)}) collective-permute-start(bf16[2,128,1408]{2,1,0:T(8,128)(2,1)} %dynamic-slice_bitcast_fusion.3), channel_id=1, source_target_pairs={{0,8},{4,12},{8,0},{12,4},{16,24},{20,28},{24,16},{28,20},{1,9},{5... | collective-permute-start | bytes 2162696 | tf_op jit(solution)/shard_map/ppermute | solution.py:57
  801.6 19.1 %collective-permute-start.92 = (bf16[2,128,1408]{2,1,0:T(8,128)(2,1)S(1)}, bf16[2,128,1408]{2,1,0:T(8,128)(2,1)S(1)}, u32[]{:S(2)}, u32[]{:S(2)}) collective-permute-start(bf16[2,128,1408]{2,1,0:T(8,128)(2,1)S(1)} %copy-done.125), channel_id=1, source_target_pairs={{0,16},{4,20},{8,24},{12,28},{16,0},{20,4},{24,8},{28,12},{1,17},{... | collective-permute-start | bytes 2162696 | tf_op jit(solution)/shard_map/ppermute | solution.py:57
  804.5 19.2 %collective-permute-start.85 = (bf16[2,128,1408]{2,1,0:T(8,128)(2,1)S(1)}, bf16[2,128,1408]{2,1,0:T(8,128)(2,1)S(1)}, u32[]{:S(2)}, u32[]{:S(2)}) collective-permute-start(bf16[2,128,1408]{2,1,0:T(8,128)(2,1)S(1)} %copy-done.126), channel_id=1, source_target_pairs={{0,8},{4,12},{8,0},{12,4},{16,24},{20,28},{24,16},{28,20},{1,9},{5... | collective-permute-start | bytes 2162696 | tf_op jit(solution)/shard_map/ppermute | solution.py:57
  807.0 29.2 %collective-permute-start.87 = (bf16[2,128,1408]{2,1,0:T(8,128)(2,1)S(1)}, bf16[2,128,1408]{2,1,0:T(8,128)(2,1)S(1)}, u32[]{:S(2)}, u32[]{:S(2)}) collective-permute-start(bf16[2,128,1408]{2,1,0:T(8,128)(2,1)S(1)} %copy-done.127), channel_id=1, source_target_pairs={{0,16},{4,20},{8,24},{12,28},{16,0},{20,4},{24,8},{28,12},{1,17},{... | collective-permute-start | bytes 2162696 | tf_op jit(solution)/shard_map/ppermute | solution.py:57
  809.3 62.3 %collective-permute-start.67 = (bf16[1024,384]{1,0:T(8,128)(2,1)}, bf16[1024,384]{1,0:T(8,128)(2,1)}, u32[]{:S(2)}, u32[]{:S(2)}) collective-permute-start(bf16[1024,384]{1,0:T(8,128)(2,1)} %convolution_convert_fusion.9), channel_id=1, source_target_pairs={{0,4},{4,0},{8,12},{12,8},{16,20},{20,16},{24,28},{28,24},{1,5},{5... | collective-permute-start | bytes 2359304 | tf_op jit(solution)/shard_map/ppermute | solution.py:57
  820.7 42.0 %collective-permute-start.96 = (bf16[704,256]{1,0:T(8,128)(2,1)}, bf16[704,256]{1,0:T(8,128)(2,1)}, u32[]{:S(2)}, u32[]{:S(2)}) collective-permute-start(bf16[704,256]{1,0:T(8,128)(2,1)} %dynamic-slice_bitcast_fusion.15), channel_id=1, source_target_pairs={{0,16},{4,20},{8,24},{12,28},{16,0},{20,4},{24,8},{28,12},{1,17},{... | collective-permute-start | bytes 1081352 | tf_op jit(solution)/shard_map/ppermute | solution.py:57
  823.7 40.1 %collective-permute-start.98 = (bf16[704,256]{1,0:T(8,128)(2,1)}, bf16[704,256]{1,0:T(8,128)(2,1)}, u32[]{:S(2)}, u32[]{:S(2)}) collective-permute-start(bf16[704,256]{1,0:T(8,128)(2,1)} %dynamic-slice_bitcast_fusion.14), channel_id=1, source_target_pairs={{0,8},{4,12},{8,0},{12,4},{16,24},{20,28},{24,16},{28,20},{1,9},{5... | collective-permute-start | bytes 1081352 | tf_op jit(solution)/shard_map/ppermute | solution.py:57
  862.7 29.5 %collective-permute-start.82 = (bf16[2,512,256]{2,1,0:T(8,128)(2,1)S(1)}, bf16[2,512,256]{2,1,0:T(8,128)(2,1)S(1)}, u32[]{:S(2)}, u32[]{:S(2)}) collective-permute-start(bf16[2,512,256]{2,1,0:T(8,128)(2,1)S(1)} %dynamic-slice_bitcast_fusion.6), channel_id=1, source_target_pairs={{0,16},{4,20},{8,24},{12,28},{16,0},{20,4},{24,8},{28,12},{1,17},{... | collective-permute-start | bytes 1572872 | tf_op jit(solution)/shard_map/ppermute | solution.py:57
  876.2 24.3 %collective-permute-start.81 = (bf16[512,256]{1,0:T(8,128)(2,1)S(1)}, bf16[512,256]{1,0:T(8,128)(2,1)S(1)}, u32[]{:S(2)}, u32[]{:S(2)}) collective-permute-start(bf16[512,256]{1,0:T(8,128)(2,1)S(1)} %dynamic-slice_bitcast_fusion.21), channel_id=1, source_target_pairs={{0,16},{4,20},{8,24},{12,28},{16,0},{20,4},{24,8},{28,12},{1,17},{... | collective-permute-start | bytes 786440 | tf_op jit(solution)/shard_map/ppermute | solution.py:57
  (256 other events, 2012.4 us)

commit v2 on v1

v2 whole, which is shorter than its diff:
```python
import functools

import jax
import jax.numpy as jnp
from jax import lax
from jax.experimental import pallas as pl
from jax.experimental.pallas import tpu as pltpu
from jax.sharding import PartitionSpec as P

HD = 256
EPS = 1e-05
ROPE_BASE = 10000.0
NEG_FILL = -1e30
BF = jnp.bfloat16
F32 = jnp.float32
VMEM_BYTES = 58 * 1024 * 1024
COST = 1e12


def dot(left, right):
    return jnp.dot(left, right, preferred_element_type=F32)


def dot_rows(left, right):
    return lax.dot_general(left, right, (((0,), (0,)), ((), ())), preferred_element_type=F32)


def dot_cols(left, right):
    return lax.dot_general(left, right, (((1,), (1,)), ((), ())), preferred_element_type=F32)


def inverse_rms(values):
    return lax.rsqrt(jnp.mean(values * values, axis=-1, keepdims=True) + EPS)


def back_norm(grad_out, unit_rows, inv_rms, gain):
    scaled = grad_out * gain
    return inv_rms * (scaled - unit_rows * jnp.mean(scaled * unit_rows, axis=-1, keepdims=True))


def turn(values, cosine, sine):
    half = HD // 2
    front, back = values[:, :half], values[:, half:]
    return front * cosine - back * sine, back * cosine + front * sine


def full_spec(shape):
    return pl.BlockSpec(tuple(shape), lambda *_: (0,) * len(shape))


def shape_of(shape, kind=BF):
    return jax.ShapeDtypeStruct(tuple(shape), kind)


def write_pieces(me, source, outs, layout):
    block = outs[0].shape[0] // len(layout[0])
    for out, rels in zip(outs, layout):
        for j, rel in enumerate(rels):
            out[j * block : (j + 1) * block, :] = source[block_rows(me ^ rel, block), :].astype(BF)


MICROS = {
    "front": 4, "query": 7, "attend": 13, "middle": 3, "ffn": 19, "mid_back": 3, "grad": 9, "attend_back": 20,
    "latent_back": 3, "ffn_sum": 3, "spread": 3, "kv_split": 3, "key_back": 3, "join": 3, "input": 8, "shared": 3,
}


def run(kernel, scalars, inputs, outputs, grid=(1,), scratch=(), name=None, carried=()):
    n_in, n_scalars = len(inputs), len(scalars)
    moved = sum(a.size * a.dtype.itemsize for a, _ in inputs)

    def body(*refs):
        kernel(*refs[: n_scalars + n_in], *refs[n_scalars + n_in + len(carried) :])

    return pl.pallas_call(
        body,
        out_shape=[s for s, _ in outputs],
        grid_spec=pltpu.PrefetchScalarGridSpec(
            num_scalar_prefetch=n_scalars,
            grid=grid,
            in_specs=[s for _, s in inputs] + [pl.BlockSpec(memory_space=pl.ANY)] * len(carried),
            out_specs=[s for _, s in outputs],
            scratch_shapes=list(scratch),
        ),
        input_output_aliases={n_scalars + n_in + k: index for k, (index, _) in enumerate(carried)},
        compiler_params=pltpu.CompilerParams(
            dimension_semantics=("arbitrary",) * len(grid), vmem_limit_bytes=VMEM_BYTES
        ),
        cost_estimate=pl.CostEstimate(flops=int(MICROS[name] * COST), bytes_accessed=moved, transcendentals=0),
        name=name,
    )(*scalars, *[a for a, _ in inputs], *[a for _, a in carried])


def total_of(refs):
    total = refs[0][...].astype(F32)
    for ref in refs[1:]:
        total = total + ref[...].astype(F32)
    return total


def row_total(refs, r, n_rows, block):
    total = 0.0
    for ref in refs:
        at = r * (ref.shape[0] // n_rows)
        total = total + ref[at : at + block, :].astype(F32)
    return total


def block_rows(index, size):
    return pl.ds(pl.multiple_of(index * size, size), size)


def front_kernel(info, x_ref, gain_ref, w_ref, cos_ref, sin_ref, n_ref, kv_ref):
    x = x_ref[0].astype(F32)
    normed = (x * inverse_rms(x) * gain_ref[...]).astype(BF)
    n_ref[...] = normed
    kv = dot(normed, w_ref[...])
    front, back = turn(kv[:, :HD], cos_ref[0], sin_ref[0])
    kv_ref[:, : HD // 2] = front.astype(BF)
    kv_ref[:, HD // 2 : HD] = back.astype(BF)
    kv_ref[:, HD:] = kv[:, HD:].astype(BF)


def query_kernel(info, n_ref, wd_ref, gain_ref, wu_ref, cos_ref, sin_ref, ln_ref, ul_ref, il_ref, q_ref, held):
    latent = dot(n_ref[...], wd_ref[...])
    inv = inverse_rms(latent)
    unit = latent * inv
    normed = (unit * gain_ref[...]).astype(BF)
    ln_ref[...] = normed
    block = ul_ref.shape[0]
    held[...] = latent
    mine = held[block_rows(info[0], block), :]
    inv_mine = inverse_rms(mine)
    ul_ref[...] = mine * inv_mine
    il_ref[...] = jnp.broadcast_to(inv_mine, il_ref.shape)
    raw = dot(normed, wu_ref[...])
    cosine, sine = cos_ref[0], sin_ref[0]
    for h in range(raw.shape[1] // HD):
        front, back = turn(raw[:, h * HD : (h + 1) * HD], cosine, sine)
        q_ref[:, h * HD : h * HD + HD // 2] = front.astype(BF)
        q_ref[:, h * HD + HD // 2 : (h + 1) * HD] = back.astype(BF)


def starts_of(docs, row, places):
    end, start = 0, jnp.zeros_like(places)
    for d in range(docs.shape[1]):
        size = docs[row, d]
        end = end + size
        start = start + jnp.where(places >= end, size, 0)
    return start


def attend_kernel(row, order, layout, info, docs, q_ref, ka_ref, kb_ref, w_ref, ctx_ref, lse_ref, *rest):
    pieces, (acc, bias) = rest[: len(layout)], rest[len(layout) :]
    h = pl.program_id(0)
    length = q_ref.shape[0]
    half = len(order) // 2 * length
    me_tp, me_seq = info[0], info[1]

    @pl.when(h == 0)
    def _():
        places = me_seq * length + lax.broadcasted_iota(jnp.int32, (length, 1), 0)
        start = starts_of(docs, row, places)
        column = lax.broadcasted_iota(jnp.int32, (1, length), 1)
        for b, rel in enumerate(order):
            key = (me_seq ^ rel) * length + column
            allowed = (key >= start) & (key <= places)
            bias[:, b * length : (b + 1) * length] = jnp.where(allowed, 0.0, NEG_FILL)

    q = q_ref[...]
    scale = HD ** (-0.5)
    sa = dot_cols(q, ka_ref[:, :HD]) * scale + bias[:, :half]
    sb = dot_cols(q, kb_ref[:, :HD]) * scale + bias[:, half:]
    peak = jnp.maximum(jnp.max(sa, axis=-1, keepdims=True), jnp.max(sb, axis=-1, keepdims=True))
    pa = jnp.exp(sa - peak)
    pb = jnp.exp(sb - peak)
    total = jnp.sum(pa, axis=-1, keepdims=True) + jnp.sum(pb, axis=-1, keepdims=True)
    out = dot(pa.astype(BF), ka_ref[:, HD:]) + dot(pb.astype(BF), kb_ref[:, HD:])
    out = (out / total).astype(BF)
    ctx_ref[...] = out
    lse = jnp.broadcast_to(peak + jnp.log(total), (length, 128))
    lse_ref[0] = jnp.transpose(lse)[:1, :]
    part = dot(out, w_ref[...])

    @pl.when(h == 0)
    def _():
        acc[...] = part

    @pl.when(h > 0)
    def _():
        acc[...] += part

    @pl.when(h == pl.num_programs(0) - 1)
    def _():
        write_pieces(me_tp, acc, pieces, layout)


def middle_kernel(info, *refs):
    parts, (x_ref, gain_ref, mid_ref, n2_ref) = refs[:-4], refs[-4:]
    mid = x_ref[0].astype(F32) + total_of(parts)
    mid_ref[...] = mid
    n2_ref[...] = (mid * inverse_rms(mid) * gain_ref[...]).astype(BF)


def place_pieces(me, pieces, out_ref, rels):
    per = len(rels) // len(pieces)
    block = pieces[0].shape[0] // per
    for i, rel in enumerate(rels):
        at = i % per * block
        out_ref[block_rows(me ^ rel, block), :] = pieces[i // per][at : at + block, :]


def ffn_kernel(n_parts, rels, layout, ff_layout, info, *refs):
    parts = refs[:n_parts]
    dy_ref, wg_hbm, wu_hbm, wd_hbm = refs[n_parts : n_parts + 4]
    outs = refs[n_parts + 4 :]
    n2_ref, hidden_ref = outs[:2]
    ff_refs, pieces = outs[2:4], outs[4 : 4 + len(layout)]
    wg, wu, wd, acc, sems = outs[4 + len(layout) :]
    me = info[0]
    width = hidden_ref.shape[2]
    step = 256
    chunks = [(i, min(step, width - i)) for i in range(0, width, step)]

    def copies(c):
        at, size = chunks[c]
        return (
            pltpu.make_async_copy(wg_hbm.at[:, pl.ds(at, size)], wg.at[:, pl.ds(at, size)], sems.at[0, c]),
            pltpu.make_async_copy(wu_hbm.at[:, pl.ds(at, size)], wu.at[:, pl.ds(at, size)], sems.at[1, c]),
            pltpu.make_async_copy(wd_hbm.at[pl.ds(at, size), :], wd.at[pl.ds(at, size), :], sems.at[2, c]),
        )

    for c in range(len(chunks)):
        for copy in copies(c):
            copy.start()
    place_pieces(me, parts, n2_ref, rels)
    n2 = n2_ref[...]
    dy = dy_ref[0]
    for c, (at, size) in enumerate(chunks):
        here = slice(at, at + size)
        for copy in copies(c):
            copy.wait()
        gate = dot(n2, wg[:, here])
        up = dot(n2, wu[:, here])
        dhid = dot_cols(dy, wd[here, :])
        sig = 1.0 / (1.0 + jnp.exp(-gate))
        swish = gate * sig
        hidden_ref[0, :, here] = (swish * up).astype(BF)
        hidden_ref[1, :, here] = (dhid * up * sig * (1.0 + gate * (1.0 - sig))).astype(BF)
        hidden_ref[2, :, here] = (dhid * swish).astype(BF)
    hid, dgate, dup = hidden_ref[0], hidden_ref[1], hidden_ref[2]
    cut = min(512, acc.shape[1])
    for at in range(0, acc.shape[1], cut):
        here = slice(at, at + cut)
        acc[:, here] = dot_cols(dgate, wg[here, :]) + dot_cols(dup, wu[here, :])
    write_pieces(me, acc, pieces, layout)
    for at in range(0, acc.shape[1], cut):
        here = slice(at, at + cut)
        acc[:, here] = dot(hid, wd[:, here])
    write_pieces(me, acc, ff_refs, ff_layout)


def mid_back_kernel(info, *refs):
    parts, (mid_ref, dy_ref, gain_ref, low_ref, dgain_ref) = refs[:-5], refs[-5:]
    d2 = total_of(parts)
    mid = mid_ref[...]
    inv = inverse_rms(mid)
    unit = mid * inv
    dgain_ref[...] = jnp.sum(d2 * unit, axis=0, keepdims=True)
    low_ref[...] = (dy_ref[0].astype(F32) + back_norm(d2, unit, inv, gain_ref[...])).astype(BF)


def attend_back_kernel(row, order, n_parts, rels, layout, info, docs, *refs):
    lows, refs = refs[:n_parts], refs[n_parts:]
    q_ref, ka_ref, kb_ref, lse_ref, wo_ref, wq_ref, cos_ref, sin_ref = refs[:8]
    low_ref, qlow_ref, keep_ref, send_ref = refs[8:12]
    pieces = refs[12:14]
    bias, dkv, lat = refs[14:]
    h = pl.program_id(0)
    length = q_ref.shape[0]
    half = len(order) // 2 * length
    me_tp, me_seq = info[0], info[1]
    scale = HD ** (-0.5)

    @pl.when(h == 0)
    def _():
        place_pieces(me_tp, lows, low_ref, rels)
        places = me_seq * length + lax.broadcasted_iota(jnp.int32, (1, length), 1)
        start = starts_of(docs, row, places)
        column = lax.broadcasted_iota(jnp.int32, (length, 1), 0)
        for b, rel in enumerate(order):
            key = (me_seq ^ rel) * length + column
            allowed = (key >= start) & (key <= places)
            bias[b * length : (b + 1) * length, :] = jnp.where(allowed, 0.0, NEG_FILL)

    q = q_ref[...]
    dctx = dot_cols(low_ref[...], wo_ref[...]).astype(BF)
    lse = lse_ref[0]
    probs, dprobs = [], []
    delta = 0.0
    for i, kv_ref in enumerate((ka_ref, kb_ref)):
        scores = dot_cols(kv_ref[:, :HD], q) * scale + bias[i * half : (i + 1) * half, :]
        prob = jnp.exp(scores - lse)
        dprob = dot_cols(kv_ref[:, HD:], dctx)
        delta = delta + jnp.sum(prob * dprob, axis=0, keepdims=True)
        probs.append(prob), dprobs.append(dprob)
    dq = 0.0
    for i, kv_ref in enumerate((ka_ref, kb_ref)):
        rows = slice(i * half, (i + 1) * half)
        dscore = (probs[i] * (dprobs[i] - delta)).astype(BF)
        dq = dq + dot_rows(dscore, kv_ref[:, :HD])
        dk = dot(dscore, q) * scale
        dv = dot(probs[i].astype(BF), dctx)

        @pl.when(h == 0)
        def _():
            dkv[rows, :HD] = dk
            dkv[rows, HD:] = dv

        @pl.when(h > 0)
        def _():
            dkv[rows, :HD] += dk
            dkv[rows, HD:] += dv

    front, back = turn(dq * scale, cos_ref[0], -sin_ref[0])
    qlow_ref[:, : HD // 2] = front.astype(BF)
    qlow_ref[:, HD // 2 :] = back.astype(BF)
    part = dot_cols(qlow_ref[...], wq_ref[...])

    @pl.when(h == 0)
    def _():
        lat[...] = part

    @pl.when(h > 0)
    def _():
        lat[...] += part

    @pl.when(h == pl.num_programs(0) - 1)
    def _():
        keep_ref[...] = dkv[:half, :].astype(BF)
        send_ref[...] = dkv[half:, :].astype(BF)
        write_pieces(me_tp, lat, pieces, layout)


def kv_split_kernel(n_rows, layout, info, *refs):
    pieces, held = refs[-3:-1], refs[-1]
    count = (len(refs) - 3) // n_rows
    rows = pieces[0].shape[0] // n_rows
    for r in range(n_rows):
        held[...] = total_of(refs[r * count : (r + 1) * count])
        outs = [piece.at[r * rows : (r + 1) * rows, :] for piece in pieces]
        write_pieces(info[0], held, outs, layout)


def latent_back_kernel(n_rows, info, *refs):
    units, invs = refs[-3 - 2 * n_rows : -3 - n_rows], refs[-3 - n_rows : -3]
    parts, (gain_ref, low_ref, dgain_ref) = refs[: -3 - 2 * n_rows], refs[-3:]
    block = low_ref.shape[0] // n_rows
    dgain = 0.0
    for r in range(n_rows):
        rows = slice(r * block, (r + 1) * block)
        unit, grad = units[r][...], row_total(parts, r, n_rows, block)
        dgain = dgain + jnp.sum(grad * unit, axis=0, keepdims=True)
        low_ref[rows, :] = back_norm(grad, unit, invs[r][:, :1], gain_ref[...]).astype(BF)
    dgain_ref[...] = dgain


def key_back_kernel(n_rows, info, *refs):
    parts, (cos_ref, sin_ref, out_ref) = refs[:-3], refs[-3:]
    block = out_ref.shape[0] // n_rows
    for r in range(n_rows):
        rows = slice(r * block, (r + 1) * block)
        total = row_total(parts, r, n_rows, block)
        front, back = turn(total[:, :HD], cos_ref[r], -sin_ref[r])
        out_ref[rows, : HD // 2] = front.astype(BF)
        out_ref[rows, HD // 2 : HD] = back.astype(BF)
        out_ref[rows, HD:] = total[:, HD:].astype(BF)


def ffn_sum_kernel(n_rows, info, *refs):
    parts, mids, out_ref = refs[: -1 - n_rows], refs[-1 - n_rows : -1], refs[-1]
    block = out_ref.shape[0] // n_rows
    for r in range(n_rows):
        out_ref[r * block : (r + 1) * block, :] = (row_total(parts, r, n_rows, block) + mids[r][...]).astype(BF)


def spread_kernel(rels, info, *refs):
    pieces, out_ref = refs[:-1], refs[-1]
    n_rows, per = out_ref.shape[0], len(rels) // len(pieces)
    block = out_ref.shape[1] // len(rels)
    for i, rel in enumerate(rels):
        for row in range(n_rows):
            at = (i % per * n_rows + row) * block
            out_ref[row, block_rows(info[0] ^ rel, block), :] = pieces[i // per][at : at + block, :]


def join_kernel(n_rows, rels, with_part, info, *refs):
    lats, kvs, outs = refs[:2], refs[2:4], refs[4:]
    me, n_tp = info[0], len(rels)
    per = n_tp // 2
    block = lats[0].shape[0] // (n_rows * per)
    lat_ref, kv_ref = outs[:2]
    for i, rel in enumerate(rels):
        for r in range(n_rows):
            rows = block_rows(r * n_tp + (me ^ rel), block)
            at = (i % per * n_rows + r) * block
            lat_ref[rows, :] = lats[i // per][at : at + block, :]
            kv_ref[rows, :] = kvs[i // per][at : at + block, :]
    if with_part:
        lat_cols, kv_cols = lat_ref.shape[1] // n_tp, kv_ref.shape[1] // n_tp
        outs[2][:, :lat_cols] = lat_ref[:, block_rows(me, lat_cols)]
        outs[2][:, lat_cols:] = kv_ref[:, block_rows(me, kv_cols)]


def input_kernel(info, lat_ref, kv_ref, x_ref, wd_ref, wkv_ref, low_ref, gain_ref, out_ref, dgain_ref):
    dn = dot_cols(lat_ref[...], wd_ref[...]) + dot_cols(kv_ref[...], wkv_ref[...])
    x = x_ref[0].astype(F32)
    inv = inverse_rms(x)
    unit = x * inv
    dgain_ref[...] = jnp.sum(dn * unit, axis=0, keepdims=True)
    out_ref[0] = (low_ref[...].astype(F32) + back_norm(dn, unit, inv, gain_ref[...])).astype(BF)


def grad_kernel(table, *refs):
    count = (len(refs) - 2) // 2
    keep_ref, send_ref = refs[2 * count :]

    def load(ref):
        value = ref[...]
        return value.reshape(-1, value.shape[-1])

    total = dot_rows(load(refs[0]), load(refs[count]))
    for i in range(1, count):
        total = total + dot_rows(load(refs[i]), load(refs[count + i]))
    total = total.astype(BF)
    i, half = pl.program_id(0), pl.num_programs(0) // 2

    @pl.when(i < half)
    def _():
        keep_ref[...] = total

    @pl.when(i >= half)
    def _():
        send_ref[...] = total


def shared_kernel(n_tp, lat_cols, kv_cols, info, *refs):
    parts, (lat_ref, kv_ref) = refs[:n_tp], refs[n_tp:]
    for r in range(n_tp):
        value = parts[r][...].astype(F32)
        lat_ref[:, block_rows(info[0] ^ r, lat_cols)] = value[:, :lat_cols]
        kv_ref[:, block_rows(info[0] ^ r, kv_cols)] = value[:, lat_cols:]


def build(n_seq, n_tp):
    seq_bits = n_seq.bit_length() - 1
    tp_bits = n_tp.bit_length() - 1

    def swap(value, axis, mask):
        count = n_seq if axis == "seq" else n_tp
        return lax.ppermute(value, axis, [(i, i ^ mask) for i in range(count)])

    def spread(bits):
        order = [0]
        for bit in bits:
            order = order + [o | (1 << bit) for o in order]
        return order

    upward = list(range(1, seq_bits))
    routes = (upward + [0], upward[::-1] + [0])
    tp_route = list(reversed(range(tp_bits)))
    tp_rels = spread(tp_route)
    halves = [tp_rels[: n_tp // 2], tp_rels[n_tp // 2 :]]
    singles = [[r] for r in range(n_tp)]
    layouts = [singles, halves]
    rels_back = [list(range(n_tp)), tp_rels]

    def gather(block):
        return [block] + [swap(block, "tp", r) for r in range(1, n_tp)]

    def shards(
        layer_in, attn_gain, query_down, latent_gain, query_up, key_value, attn_out,
        ffn_gain, gate_proj, up_proj, down_proj, out_grad, doc_lengths,
    ):
        n_rows, length, model_dim = layer_in.shape
        lat_dim, q_width = query_up.shape
        ff_dim = gate_proj.shape[1]
        heads = q_width // HD
        block = length // n_tp
        half_keys = n_seq // 2 * length
        rows = range(n_rows)
        seq_me, tp_me = lax.axis_index("seq"), lax.axis_index("tp")
        state = [jnp.stack([tp_me, seq_me, jnp.zeros_like(tp_me)]).astype(jnp.int32)]
        me_bits = [(seq_me >> b) & 1 for b in range(seq_bits)]
        last, due = [], []

        def wait(*arrays):
            due.extend(arrays)

        def after(value):
            ready = last[-1:] + due
            due.clear()
            return lax.optimization_barrier((value, *ready))[0] if ready else value

        def step(kernel, inputs, outputs, table=None, docs=False, **kw):
            scalars = (after(state[0] if table is None else table),) + ((doc_lengths,) if docs else ())
            out = run(kernel, scalars, inputs, outputs, **kw)
            last.append(min(out, key=lambda o: o.size))
            return out

        def total(values, kind):
            out = after(values[-1][0])[values[-1][1]].astype(F32)
            for array, index in values[:-1]:
                out = out + array[index].astype(F32)
            out = out.astype(kind)
            last.append(out)
            return out

        def add(parts, rows, at, kind):
            return total([(p, slice(at * rows, (at + 1) * rows)) for p in parts], kind)

        def halve(parts, rows, axis, bit):
            half = rows // 2
            return parts + [swap(add(parts, half, 1, BF), axis, 1 << bit)], half

        def halve_all(parts, rows, axis, bits):
            for bit in reversed(bits):
                parts, rows = halve(parts, rows, axis, bit)
            return parts, rows

        places = seq_me * length + jnp.arange(length, dtype=jnp.int32)
        ends = jnp.cumsum(doc_lengths, axis=1)
        passed = places[None, :, None] >= ends[:, None, :]
        inner = places[None, :] - jnp.sum(jnp.where(passed, doc_lengths[:, None, :], 0), axis=-1)
        frequency = ROPE_BASE ** (-jnp.arange(HD // 2, dtype=F32) / (HD // 2))
        angles = inner.astype(F32)[:, :, None] * frequency
        cosine, sine = jnp.cos(angles), jnp.sin(angles)
        gain_row = lambda gain: (gain.reshape(1, -1), full_spec((1, gain.shape[0])))

        def whole(array):
            return array, full_spec(array.shape)

        def first(array, count):
            return array, full_spec((count, array.shape[1]))

        def row_of(array, r):
            return array, pl.BlockSpec((1,) + array.shape[1:], lambda *_: (r, 0, 0))

        def own_of(array, r):
            shape = (1, block, array.shape[2])
            return array, pl.BlockSpec(shape, lambda i, info, *_: (r, info[0], 0))

        def new(shape, kind=BF):
            return shape_of(shape, kind), full_spec(shape)

        def head_cols(array):
            return array, pl.BlockSpec((array.shape[0], HD), lambda h, *_: (0, h))

        def head_rows(array):
            return array, pl.BlockSpec((HD, array.shape[1]), lambda h, *_: (h, 0))

        def row_pieces(r, width):
            rows_out = n_tp // 2 * block
            spec = pl.BlockSpec((rows_out, width), lambda *_: (r, 0))
            return [(shape_of((n_rows * rows_out, width)), spec)] * 2

        def pieces_of(layout, width):
            return [new((len(rels) * block, width)) for rels in layout]

        hbm = pl.BlockSpec(memory_space=pl.ANY)
        chunks = -(-ff_dim // 256)

        def rows_of(width, r, spec=None):
            return shape_of((n_rows * length, width)), spec or pl.BlockSpec((length, width), lambda *_: (r, 0))

        def row_block(array, r):
            return array, pl.BlockSpec((length, array.shape[1]), lambda *_: (r, 0))

        def going(held, *pairs):
            return [(index, held[key]) for index, key in pairs] if held else []

        def front(r, held):
            return step(
                front_kernel,
                [row_of(layer_in, r), gain_row(attn_gain), whole(key_value), row_of(cosine, r), row_of(sine, r)],
                [rows_of(model_dim, r), new((length, 2 * HD))], name="front", carried=going(held, (0, 0)),
            )

        def query(r, held):
            return step(
                query_kernel,
                [row_block(normed, r), whole(query_down), gain_row(latent_gain), whole(query_up),
                 row_of(cosine, r), row_of(sine, r)],
                [rows_of(lat_dim, r), new((block, lat_dim), F32), new((block, 128), F32), new((length, q_width))],
                scratch=[pltpu.VMEM((length, lat_dim), F32)], name="query", carried=going(held, (0, 0)),
            )

        def attend(r, held):
            return step(
                functools.partial(attend_kernel, r, spread(routes[r % 2]), layouts[r]),
                [head_cols(queries[r]), whole(near[r]), whole(far[r]), head_rows(attn_out)],
                [
                    rows_of(q_width, r, pl.BlockSpec((length, HD), lambda h, *_: (r, h))),
                    (shape_of((heads, 1, length), F32), pl.BlockSpec((1, 1, length), lambda h, *_: (h, 0, 0))),
                ] + pieces_of(layouts[r], model_dim),
                docs=True, grid=(heads,),
                scratch=[pltpu.VMEM((length, model_dim), F32), pltpu.VMEM((length, 2 * half_keys), F32)],
                name="attend", carried=going(held, (0, 0)),
            )

        def mid_step(r, parts):
            return step(
                middle_kernel, [first(p, block) for p in parts] + [own_of(layer_in, r), gain_row(ffn_gain)],
                [new((block, model_dim), F32), new((block, model_dim))], name="middle",
            )

        def ffn(r, held):
            return step(
                functools.partial(ffn_kernel, len(normed2[r]), range(n_tp), layouts[r], halves),
                [whole(p) for p in normed2[r]] + [row_of(out_grad, r),
                 (gate_proj, hbm), (up_proj, hbm), (down_proj, hbm)],
                [rows_of(model_dim, r),
                 (shape_of((3, n_rows * length, ff_dim)), pl.BlockSpec((3, length, ff_dim), lambda *_: (0, r, 0)))]
                + row_pieces(r, model_dim) + pieces_of(layouts[r], model_dim),
                scratch=[
                    pltpu.VMEM((model_dim, ff_dim), BF), pltpu.VMEM((model_dim, ff_dim), BF),
                    pltpu.VMEM((ff_dim, model_dim), BF), pltpu.VMEM((length, model_dim), F32),
                    pltpu.SemaphoreType.DMA((3, chunks)),
                ],
                name="ffn", carried=going(held, *[(i, i) for i in range(4)]),
            )

        def mid_back(r, parts):
            return step(
                mid_back_kernel,
                [first(p, block) for p in parts] + [whole(middle[r]), own_of(out_grad, r), gain_row(ffn_gain)],
                [new((block, model_dim)), new((1, model_dim), F32)], name="mid_back",
            )

        def attend_back(r, held):
            return step(
                functools.partial(attend_back_kernel, r, spread(routes[r % 2]), len(mid_low[r]), rels_back[r], halves),
                [whole(p) for p in mid_low[r]]
                + [head_cols(queries[r]), whole(near[r]), whole(far[r]),
                   (lse[r], pl.BlockSpec((1, 1, length), lambda h, *_: (h, 0, 0))),
                   head_rows(attn_out), head_cols(query_up), row_of(cosine, r), row_of(sine, r)],
                [rows_of(model_dim, r), rows_of(q_width, r, pl.BlockSpec((length, HD), lambda h, *_: (r, h))),
                 new((half_keys, 2 * HD)), new((half_keys, 2 * HD))] + row_pieces(r, lat_dim),
                docs=True, grid=(heads,),
                scratch=[pltpu.VMEM((2 * half_keys, length), F32), pltpu.VMEM((2 * half_keys, 2 * HD), F32),
                         pltpu.VMEM((length, lat_dim), F32)],
                name="attend_back", carried=going(held, (0, 0), (1, 1), (4, 4), (5, 5)),
            )

        def halve_rows(parts, count):
            half = count // 2 * block
            width = parts[0].shape[1]
            values = [(p.reshape(n_rows, -1, width), (slice(None), slice(half, 2 * half))) for p in parts]
            away = total(values, BF).reshape(n_rows * half, width)
            return parts + [swap(away, "tp", 1 << tp_route[count.bit_length() - 2])]

        def joined_pair(held):
            pair = jnp.concatenate([after(held[0]), held[1]], axis=0)
            last.append(pair)
            return pair

        def gather_start(piece):
            return piece, swap(piece, "tp", 1 << tp_route[0])

        def gather_end(held):
            for bit in tp_route[1:]:
                held = joined_pair(held)
                held = held, swap(held, "tp", 1 << bit)
            return list(held)

        def both(array):
            return [array, swap(array, "seq", 1)]

        def weight_grad(acts, deltas, by_cols, route):
            acts, deltas = [[a if isinstance(a, tuple) else (a, None) for a in pair] for pair in (acts, deltas)]
            bits = routes[route][:-1]
            order = [o for o in spread(bits)]
            count = n_seq // 2
            size = (deltas if by_cols else acts)[0][0].shape[-1] // n_seq
            if size % 128:
                flat = [jnp.concatenate([a for a, _ in pair], axis=0) for pair in (acts, deltas)]
                full = dot_rows(*flat).astype(BF)
                blocks = jnp.take(full.reshape(n_seq, -1, full.shape[1]), jnp.stack([seq_me ^ o for o in order]), axis=0)
                parts, left = halve([blocks.reshape(-1, full.shape[1])], count * size, "seq", bits[-1])
            else:

                def operands(arrays, cut):
                    out = []
                    for array, which in arrays:
                        lead = array.shape[:-1]
                        if which is not None:
                            out.append((array, pl.BlockSpec((1,) + array.shape[1:], lambda i, t: (which, 0, 0))))
                        elif cut:
                            zeros = (0,) * len(lead)
                            out.append((array, pl.BlockSpec(lead + (size,), lambda i, t, z=zeros: z + (t[i],))))
                        else:
                            out.append(whole(array))
                    return out

                shape = (acts[0][0].shape[-1], size) if by_cols else (size, deltas[0][0].shape[-1])
                half = count // 2
                part = shape_of((half * shape[0], shape[1]))
                keep, away = step(
                    grad_kernel, operands(acts, not by_cols) + operands(deltas, by_cols),
                    [(part, pl.BlockSpec(shape, lambda i, t: (jnp.minimum(i, half - 1), 0))),
                     (part, pl.BlockSpec(shape, lambda i, t: (jnp.maximum(i - half, 0), 0)))],
                    table=jnp.stack([seq_me ^ o for o in order]).astype(jnp.int32), grid=(count,), name="grad",
                )
                parts, left = [keep, swap(away, "seq", 1 << bits[-1])], keep.shape[0]
            yield parts[-1]
            parts, left = halve_all(parts, left, "seq", bits[:-1])
            yield parts[-1]
            yield add(parts, left, 0, F32)

        dy_both = both(out_grad)
        held, out = [], None
        for r in rows:
            out = front(r, out)
            held.append([out[1], swap(out[1], "seq", 1 << routes[r % 2][0])])
        normed = out[0]
        normed_both = both(normed)
        unit_lat, inv_lat, queries = [], [], []

        def widen(r, bit):
            pair = joined_pair(held[r])
            held[r] = [pair, swap(pair, "seq", 1 << bit)]

        out = None
        for r in rows:
            out = query(r, out)
            unit_lat.append(out[1]), inv_lat.append(out[2]), queries.append(out[3])
            if r == 0:
                wait(dy_both[1], normed_both[1])
                for bit in range(1, seq_bits - 1):
                    for k in rows:
                        widen(k, routes[k % 2][bit])
        latent_norm = out[0]
        latent_both = both(latent_norm)
        near, far = [None] * n_rows, [None] * n_rows
        for r in rows:
            widen(r, 0)
            near[r], far[r] = held[r]
        wait(latent_both[1])
        lse, part1, out = [], [], None

        def sent_over(pieces):
            if len(pieces) == 2:
                return [pieces[0], swap(pieces[1], "tp", 1)]
            return [pieces[0]] + [swap(pieces[r], "tp", r) for r in range(1, n_tp)]

        for r in rows:
            out = attend(r, out)
            lse.append(out[1])
            part1.append(sent_over(out[2:]))
        context = out[0]
        context_both = both(context)
        sent = n_tp // 2 * block
        middle, normed2 = [], []
        mid, n2 = mid_step(0, part1[0])
        middle.append(mid)
        normed2.append(gather(n2))
        wait(context_both[1])
        part1[1], _ = halve_all(part1[1], sent, "tp", tp_route[:-1])
        wait(*normed2[0])
        mid, n2 = mid_step(1, part1[1])
        middle.append(mid)
        normed2.append(gather(n2))

        part2, out = [], None
        for r in rows:
            out = ffn(r, out)
            part2.append(sent_over(out[4:]))
        n2_all, hidden, ffn_keep, ffn_send = out[:4]
        hidden_both = both(hidden)
        pick = lambda k: [(h, k) for h in hidden_both]
        mid_low, dgain_mid = [], []
        low, dg = mid_back(0, part2[0])
        mid_low.append(gather(low)), dgain_mid.append(dg)
        wait(hidden_both[1])
        part2[1], _ = halve_all(part2[1], sent, "tp", tp_route[:-1])
        n2_both = both(after(n2_all))
        grad_down = weight_grad(pick(0), dy_both, True, 0)
        grad_gate = weight_grad(n2_both, pick(1), False, 1)
        grad_up = weight_grad(n2_both, pick(2), False, 0)
        down_2 = next(grad_down)
        gate_2 = next(grad_gate)
        low, dg = mid_back(1, part2[1])
        wait(*mid_low[0])
        mid_low.append(gather_start(after(low))), dgain_mid.append(dg)

        kv_parts = []
        out = attend_back(0, None)
        kv_parts.append(([out[2], swap(out[3], "seq", 1 << routes[0][-1])], half_keys))
        wait(down_2)
        mid_low[1] = gather_end(mid_low[1])
        up_2 = next(grad_up)
        kv_parts[0] = halve(*kv_parts[0], "seq", routes[0][-2])
        ffn_parts = [ffn_keep, swap(after(ffn_send), "tp", 1)]
        wait(gate_2)
        out = attend_back(1, out)
        low_all, query_low = out[:2]
        kv_parts.append(([out[2], swap(out[3], "seq", 1 << routes[1][-1])], half_keys))
        lat_parts = [out[4], swap(out[5], "tp", 1)]
        kv_parts[0] = halve_all(*kv_parts[0], "seq", routes[0][:-2])
        wait(ffn_parts[1])
        kv_parts[1] = halve(*kv_parts[1], "seq", routes[1][-2])
        for count in [n_tp >> i for i in range(1, tp_bits)]:
            ffn_parts = halve_rows(ffn_parts, count)
        wait(up_2)
        for count in [n_tp >> i for i in range(1, tp_bits)]:
            lat_parts = halve_rows(lat_parts, count)
        low_both = both(after(low_all))
        wait(kv_parts[0][0][-1])
        grad_out = weight_grad(context_both, low_both, True, 1)
        out_2 = next(grad_out)
        kv_parts[1] = halve_all(*kv_parts[1], "seq", routes[1][:-2])
        query_low_both = both(after(query_low))
        lat_low, dgain_lat = step(
            functools.partial(latent_back_kernel, n_rows),
            [whole(p) for p in lat_parts] + [whole(u) for u in unit_lat] + [whole(i) for i in inv_lat]
            + [gain_row(latent_gain)],
            [new((n_rows * block, lat_dim)), new((1, lat_dim), F32)], name="latent_back",
        )
        lat_blocks = gather_start(lat_low)
        grad_query = weight_grad(latent_both, query_low_both, False, 0)
        query_2 = next(grad_query)
        wait(ffn_parts[-1])
        kv_parts = step(
            functools.partial(kv_split_kernel, n_rows, halves),
            [first(p, length) for parts, _ in kv_parts for p in parts],
            [new((n_rows * sent, 2 * HD))] * 2,
            scratch=[pltpu.VMEM((length, 2 * HD), F32)], name="kv_split",
        )
        kv_parts = [kv_parts[0], swap(kv_parts[1], "tp", 1)]
        ffn_own = step(
            functools.partial(ffn_sum_kernel, n_rows), [whole(p) for p in ffn_parts] + [whole(m) for m in middle],
            [new((n_rows * block, model_dim))], name="ffn_sum",
        )[0]
        lat_blocks = gather_end(lat_blocks)
        ffn_blocks = gather_start(after(ffn_own))
        wait(out_2)
        for count in [n_tp >> i for i in range(1, tp_bits)]:
            kv_parts = halve_rows(kv_parts, count)
        down_3 = next(grad_down)
        wait(query_2)
        gate_3 = next(grad_gate)
        own_rows = pl.BlockSpec((n_rows, block, HD // 2), lambda i, info, *_: (0, info[0], 0))
        kv_low = step(
            functools.partial(key_back_kernel, n_rows),
            [whole(p) for p in kv_parts] + [(cosine, own_rows), (sine, own_rows)],
            [new((n_rows * block, 2 * HD))], name="key_back",
        )[0]
        kv_blocks = gather_start(kv_low)
        wait(down_3)
        up_3 = next(grad_up)
        wait(ffn_blocks[1])
        down_grad = next(grad_down)
        kv_blocks = gather_end(kv_blocks)
        wait(gate_3)
        ffn_blocks = gather_end(ffn_blocks)
        out_3 = next(grad_out)
        wait(up_3)
        query_3 = next(grad_query)

        lat_cols, kv_cols = lat_dim // n_tp, 2 * HD // n_tp
        with_part = kv_cols % 128 == 0
        joined = step(
            functools.partial(join_kernel, n_rows, tp_rels, with_part),
            [whole(p) for p in lat_blocks] + [whole(p) for p in kv_blocks],
            [new((n_rows * length, lat_dim)), new((n_rows * length, 2 * HD))]
            + ([new((n_rows * length, lat_cols + kv_cols))] if with_part else []),
            name="join",
        )
        lat_all, kv_all = joined[:2]
        if with_part:
            delta = joined[2]
        else:
            delta = jnp.concatenate(
                [lax.dynamic_slice_in_dim(lat_all, tp_me * lat_cols, lat_cols, 1),
                 lax.dynamic_slice_in_dim(kv_all, tp_me * kv_cols, kv_cols, 1)], axis=1)
        delta_both = both(delta)
        dgain_in = []

        def input_step(r, held):
            out = step(
                input_kernel,
                [row_block(lat_all, r), row_block(kv_all, r), row_of(layer_in, r), whole(query_down), whole(key_value),
                 row_block(low_all, r), gain_row(attn_gain)],
                [(shape_of(layer_in.shape), pl.BlockSpec((1, length, model_dim), lambda *_: (r, 0, 0))),
                 new((1, model_dim), F32)],
                name="input", carried=going(held, (0, 0)),
            )
            dgain_in.append(out[1])
            return out

        wait(out_3, query_3)
        gate_grad = next(grad_gate)
        grad_shared = weight_grad(normed_both, delta_both, False, 0)
        shared_2 = next(grad_shared)
        out = input_step(0, None)
        wait(shared_2)
        shared_3 = next(grad_shared)
        input_grad = input_step(1, out)[0]
        wait(shared_3)

        own_dim = model_dim // n_seq
        shared = gather(next(grad_shared).astype(BF))

        gains = jnp.concatenate(
            [
                jnp.where(tp_me == 0, sum(dgain_in), 0.0).reshape(n_seq, -1),
                sum(dgain_mid).reshape(n_seq, -1),
                dgain_lat.reshape(n_seq, -1),
            ],
            axis=1,
        )
        for bit in range(seq_bits):
            pairs = gains.reshape(-1, 2, gains.shape[-1])
            flip = lax.dynamic_index_in_dim(pairs, 1 - me_bits[bit], 1, keepdims=False)
            mine = lax.dynamic_index_in_dim(pairs, me_bits[bit], 1, keepdims=False)
            gains = mine + swap(flip, "seq", 1 << bit)
        for bit in range(tp_bits):
            gains = gains + swap(gains, "tp", 1 << bit)
        gains = gains[0]
        up_grad, out_weight_grad, query_up_grad = next(grad_up), next(grad_out), next(grad_query)
        layer_out = step(
            functools.partial(spread_kernel, tp_rels), [whole(p) for p in ffn_blocks], [new(layer_in.shape)],
            name="spread",
        )[0]
        if not with_part:
            blocks = jnp.take(jnp.stack(shared), jnp.stack([tp_me ^ r for r in range(n_tp)]), axis=0).astype(F32)
            down_q = blocks[:, :, :lat_cols].transpose(1, 0, 2).reshape(own_dim, lat_dim)
            kv_grad = blocks[:, :, lat_cols:].transpose(1, 0, 2).reshape(own_dim, 2 * HD)
        else:
            down_q, kv_grad = step(
                functools.partial(shared_kernel, n_tp, lat_cols, kv_cols), [whole(p) for p in shared],
                [new((own_dim, lat_dim), F32), new((own_dim, 2 * HD), F32)], name="shared",
            )
        return (
            layer_out, input_grad, gains[:own_dim], down_q, gains[2 * own_dim :], query_up_grad,
            kv_grad, out_weight_grad.reshape(q_width, own_dim), gains[own_dim : 2 * own_dim], gate_grad, up_grad,
            down_grad.reshape(ff_dim, own_dim),
        )

    return shards


def solution(mesh):
    return jax.shard_map(
        build(mesh.shape["seq"], mesh.shape["tp"]),
        mesh=mesh,
        in_specs=(
            P(None, "seq", None), P(), P(), P(), P(None, "tp"), P(), P("tp", None), P(),
            P(None, "tp"), P(None, "tp"), P("tp", None), P(None, "seq", None), P(),
        ),
        out_specs=(
            P(None, "seq", None), P(None, "seq", None), P("seq"), P("seq", None), P("seq"),
            P("seq", "tp"), P("seq", None), P("tp", "seq"), P("seq"), P("seq", "tp"),
            P("seq", "tp"), P("tp", "seq"),
        ),
        check_vma=False,
    )
```

time: 927 us -> 578 us (0.62)
  Pallas kernels: 0 us -> 224 us
  local copies, waits for them, and re-layouts: 223 us -> 25.1 us
  matrix products: 155 us -> 0 us
  other arithmetic: 128 us -> 44.4 us
  waiting for transfers between devices: 278 us -> 200 us
  starting transfers between devices: 125 us -> 72.5 us
    pallas_call x0 -> x29, Pallas kernels: none -> 224 us  [run(): pl.pallas_call(body, out_shape=[s for s, _ in outputs], grid_spec=pltpu.P...]
    dot_general x52 -> x0, matrix products: 155 us -> none  [the longest x18 66.4 us: dot_cols(): lax.dot_general(left, right, (((1,), (1,)), ((), ())), preferred_element_...]
    ppermute x99 -> x74, waiting for transfers between devices: 278 us -> 200 us  [swap(): return lax.ppermute(value, axis, [(i, i ^ mask) for i in range(count)])]
    ppermute x99 -> x74, starting transfers between devices: 125 us -> 72.5 us  [swap(): return lax.ppermute(value, axis, [(i, i ^ mask) for i in range(count)])]
    unnamed x450 -> x120, local copies, waits for them, and re-layouts: 62.4 us -> 12.6 us
    dynamic_slice x14 -> x2, local copies, waits for them, and re-layouts: 43.7 us -> 0.04 us  [shards(): mine = lax.dynamic_index_in_dim(pairs, me_bits[bit], 1, keepdims=False)]
    another operation x54 -> x4, other arithmetic: 29.8 us -> 2.68 us  [the longest x2 1.17 us: weight_grad(): jnp.stack([seq_me ^ o for o in order]).astype(jnp.int32)]
    convert_element_type x6 -> x0, local copies, waits for them, and re-layouts: 19.9 us -> none  [the longest x4 16.5 us: shards(): x = layer_in[r].astype(F32)]
  transfers between devices with their start and end apart: 99 -> 74, of which waited for: 51 -> 30; matrix products, arithmetic and copies ran while one was open for 50% -> 10% of each run, Pallas kernels for 0% -> 35%
where the time goes in v2:
time: 578 us; the launch traced here: 568 us
  Pallas kernels  224 us (39%)
  waiting for transfers between devices  200 us (35%)
  starting transfers between devices  72.5 us (13%)
  other arithmetic  44.4 us (8%)
  local copies, waits for them, and re-layouts  25.1 us (4%)
    pallas_call x29, Pallas kernels, run(): pl.pallas_call(body, out_shape=[s for s, _ in outputs], grid_spec=pltpu.P...  224 us
    ppermute x74, waiting for transfers between devices, swap(): return lax.ppermute(value, axis, [(i, i ^ mask) for i in range(count)])  200 us
    ppermute x74, starting transfers between devices, swap(): return lax.ppermute(value, axis, [(i, i ^ mask) for i in range(count)])  72.5 us
    convert_element_type x15, other arithmetic, total(): out = out.astype(kind)  24.6 us
    add x6, other arithmetic, total(): out = out + array[index].astype(F32)  13.7 us
    unnamed x120, local copies, waits for them, and re-layouts  12.6 us
  transfers between devices with their start and end apart: 74, of which 30 were waited for; matrix products, arithmetic and copies ran while one was open for 10% of the time, Pallas kernels for 35%

profile of v2, /device:TPU:0, one launch (start us, length us, event | category | flops | bytes accessed | tf_op | source)
XLA Modules:
  0.0 567.5 jit_solution(14800158785548295393)
XLA Ops:
  4.8 4.3 front.2
  12.1 4.3 front.3
  18.4 6.7 %query.2 = (bf16[512,1024]{1,0:T(8,128)(2,1)}, f32[64,1024]{1,0:T(8,128)}, f32[64,128]{1,0:T(8,128)}, bf16[256,1024]{1,0:T(8,128)(2,1)}) custom-call(s32[3]{0:T(128)} %pad_add_fusion.refs_0_, bf16[512,2048]{1,0:T(8,128)(2,1)} %get-tuple-element.161.refs_1_, bf16[2048,1024]{1,0:T(8,128)(2,1)} %refs_4_.9, f32[1,1024]{1,0:T(1,128)} %bitcast.50, ...), custom_call_target="tpu_custom_call" | custom-call | flops 6999999774720 | bytes 8916992 | tf_op jit(solution)/shard_map/query/pallas_call | solution.py:75
  30.5 6.6 %query.3 = (bf16[512,1024]{1,0:T(8,128)(2,1)}, f32[64,1024]{1,0:T(8,128)}, f32[64,128]{1,0:T(8,128)}, bf16[256,1024]{1,0:T(8,128)(2,1)}) custom-call(s32[3]{0:T(128)} %pad_add_fusion.refs_0_, bf16[512,2048]{1,0:T(8,128)(2,1)} %get-tuple-element.161.refs_1_, bf16[2048,1024]{1,0:T(8,128)(2,1)} %refs_4_.9, ...), custom_call_target="tpu_custom_call", output_to_operand_aliasing={{0}: (7, {})} | custom-call | flops 6999999774720 | bytes 8916992 | tf_op jit(solution)/shard_map/query/pallas_call | solution.py:75
  38.1 3.3 collective-permute-done.4
  45.1 12.0 %collective-permute-done.5 = bf16[512,512]{1,0:T(8,128)(2,1)S(1)} collective-permute-done((bf16[512,512]{1,0:T(8,128)(2,1)}, bf16[512,512]{1,0:T(8,128)(2,1)S(1)}, u32[]{:S(2)}, u32[]{:S(2)}) %collective-permute-start.5) | collective-permute-done | bytes 524320 | tf_op jit(solution)/shard_map/ppermute | solution.py:461
  59.9 13.0 %attend.2 = (bf16[512,1024]{1,0:T(8,128)(2,1)}, f32[4,1,256]{2,1,0:T(1,128)}, bf16[64,2048]{1,0:T(8,128)(2,1)}, bf16[64,2048]{1,0:T(8,128)(2,1)}, bf16[64,2048]{1,0:T(8,128)(2,1)}, /*index=5*/bf16[64,2048]{1,0:T(8,128)(2,1)}) custom-call(s32[3]{0:T(128)} %pad_add_fusion.refs_0_, s32[2,8]{1,0:T(2,128)} %refs_1_.11, ...), custom_call_target="tpu_custom_call" | custom-call | flops 12999999881216 | bytes 6815744 | tf_op jit(solution)/shard_map/attend/pallas_call | solution.py:75
  77.4 13.1 %attend.3 = (bf16[512,1024]{1,0:T(8,128)(2,1)}, f32[4,1,256]{2,1,0:T(1,128)}, bf16[128,2048]{1,0:T(8,128)(2,1)}, bf16[128,2048]{1,0:T(8,128)(2,1)}) custom-call(s32[3]{0:T(128)} %pad_add_fusion.refs_0_, s32[2,8]{1,0:T(2,128)} %refs_1_.11, bf16[256,1024]{1,0:T(8,128)(2,1)} %get-tuple-element.175.refs_2_.refs_4_, ...), custom_call_target="tpu_custom_call", output_to_operand_aliasing={{0}: (6, {})} | custom-call | flops 12999999881216 | bytes 6815744 | tf_op jit(solution)/shard_map/attend/pallas_call | solution.py:75
  91.4 4.8 collective-permute-done.11.refs_3_
  96.2 3.2 middle.2
  99.4 5.5 collective-permute-start.14
  111.6 5.5 collective-permute-done.14.refs_2_
  117.2 14.9 %collective-permute-done.15.refs_3_ = bf16[64,2048]{1,0:T(8,128)(2,1)S(1)} collective-permute-done((bf16[64,2048]{1,0:T(8,128)(2,1)}, bf16[64,2048]{1,0:T(8,128)(2,1)S(1)}, u32[]{:S(2)}, u32[]{:S(2)}) %collective-permute-start.15) | collective-permute-done | bytes 262176 | tf_op jit(solution)/shard_map/ppermute | solution.py:461
  132.1 9.4 %collective-permute-done.17.refs_3_ = bf16[64,2048]{1,0:T(8,128)(2,1)S(1)} collective-permute-done((bf16[64,2048]{1,0:T(8,128)(2,1)S(1)}, bf16[64,2048]{1,0:T(8,128)(2,1)S(1)}, u32[]{:S(2)}, u32[]{:S(2)}) %collective-permute-start.17) | collective-permute-done | bytes 262176 | tf_op jit(solution)/shard_map/ppermute | solution.py:461
  145.1 3.0 collective-permute-start.19
  149.5 19.3 %ffn.2 = (bf16[512,2048]{1,0:T(8,128)(2,1)}, bf16[3,512,1408]{2,1,0:T(8,128)(2,1)}, bf16[256,2048]{1,0:T(8,128)(2,1)}, bf16[256,2048]{1,0:T(8,128)(2,1)}, bf16[6...) custom-call(s32[3]{0:T(128)} %pad_add_fusion.refs_0_, ...), custom_call_target="tpu_custom_call" | custom-call | flops 18999999987712 | bytes 20447232 | tf_op jit(solution)/shard_map/ffn/pallas_call | solution.py:75
  168.9 3.0 collective-permute-start.23
  173.3 19.7 %ffn.3 = (bf16[512,2048]{1,0:T(8,128)(2,1)}, bf16[3,512,1408]{2,1,0:T(8,128)(2,1)}, bf16[256,2048]{1,0:T(8,128)(2,1)}, bf16[256,2048]{1,0:T(8,128)(2,1)}, bf16[1...) custom-call(s32[3]{0:T(128)} %pad_add_fusion.refs_0_, ...), custom_call_target="tpu_custom_call", output_to_operand_aliasing={{0}: (9, {}), {1}: (10, {}), {2}: (11, {}), {3}: (12, {})} | custom-call | flops 18999999987712 | bytes 20447232 | tf_op jit(solution)/shard_map/ffn/pallas_call | solution.py:75
  193.2 3.5 mid_back.2
  201.1 12.7 %collective-permute-done.21.refs_2_ = bf16[128,2048]{1,0:T(8,128)(2,1)} collective-permute-done((bf16[128,2048]{1,0:T(8,128)(2,1)}, bf16[128,2048]{1,0:T(8,128)(2,1)}, u32[]{:S(2)}, u32[]{:S(2)}) %collective-permute-start.21) | collective-permute-done | bytes 524320 | tf_op jit(solution)/shard_map/ppermute | solution.py:461
  216.1 8.2 %grad.6 = (bf16[2816,256]{1,0:T(8,128)(2,1)}, bf16[2816,256]{1,0:T(8,128)(2,1)}) custom-call(s32[4]{0:T(128)} %add_add_fusion.refs_0_, bf16[3,512,1408]{2,1,0:T(8,128)(2,1)} %get-tuple-element.206.refs_1_.refs_3_, bf16[3,512,1408]{2,1,0:T(8,128)(2,1)} %collective-permute-done.25.refs_2_.refs_4_, bf16[2,256,2048]{2,1,0:T(8,128)(2,1)} %refs_5_.13, ...), custom_call_target="tpu_custom_call" | custom-call | flops 9000000159744 | bytes 12845056 | tf_op jit(solution)/shard_map/grad/pallas_call | solution.py:75
  225.1 8.5 %grad.7 = (bf16[512,1408]{1,0:T(8,128)(2,1)}, bf16[512,1408]{1,0:T(8,128)(2,1)}) custom-call(s32[4]{0:T(128)} %add_add_fusion.1.refs_0_, bf16[512,2048]{1,0:T(8,128)(2,1)} %get-tuple-element.212.refs_1_, bf16[512,2048]{1,0:T(8,128)(2,1)} %collective-permute-done.26.refs_2_, bf16[3,512,1408]{2,1,0:T(8,128)(2,1)} %get-tuple-element.206.refs_1_.refs_3_, ...), custom_call_target="tpu_custom_call" | custom-call | flops 9000000159744 | bytes 12845056 | tf_op jit(solution)/shard_map/grad/pallas_call | solution.py:75
  236.5 3.2 mid_back.3
  239.8 20.2 %attend_back.2 = (bf16[512,2048]{1,0:T(8,128)(2,1)}, bf16[512,1024]{1,0:T(8,128)(2,1)}, bf16[1024,512]{1,0:T(8,128)(2,1)}, bf16[1024,512]{1,0:T(8,128)(2,1)}, bf...) custom-call(s32[3]{0:T(128)} %pad_add_fusion.refs_0_, s32[2,8]{1,0:T(2,128)} %refs_1_.11, ...), custom_call_target="tpu_custom_call" | custom-call | flops 19999999655936 | bytes 10489856 | tf_op jit(solution)/shard_map/attend_back/pallas_call | solution.py:75
  265.7 8.5 %grad.8 = (bf16[512,1408]{1,0:T(8,128)(2,1)}, bf16[512,1408]{1,0:T(8,128)(2,1)}) custom-call(s32[4]{0:T(128)} %add_add_fusion.refs_0_, bf16[512,2048]{1,0:T(8,128)(2,1)} %get-tuple-element.212.refs_1_, bf16[512,2048]{1,0:T(8,128)(2,1)} %collective-permute-done.26.refs_2_, bf16[3,512,1408]{2,1,0:T(8,128)(2,1)} %get-tuple-element.206.refs_1_.refs_3_, ...), custom_call_target="tpu_custom_call" | custom-call | flops 9000000159744 | bytes 12845056 | tf_op jit(solution)/shard_map/grad/pallas_call | solution.py:75
  276.2 18.3 %collective-permute-done.34 = bf16[512,1408]{1,0:T(8,128)(2,1)} collective-permute-done((bf16[512,1408]{1,0:T(8,128)(2,1)}, bf16[512,1408]{1,0:T(8,128)(2,1)}, u32[]{:S(2)}, u32[]{:S(2)}) %collective-permute-start.34) | collective-permute-done | bytes 1441824 | tf_op jit(solution)/shard_map/ppermute | solution.py:461
  294.5 20.2 %attend_back.3 = (bf16[512,2048]{1,0:T(8,128)(2,1)}, bf16[512,1024]{1,0:T(8,128)(2,1)}, bf16[1024,512]{1,0:T(8,128)(2,1)}, bf16[1024,512]{1,0:T(8,128)(2,1)}, bf...) custom-call(s32[3]{0:T(128)} %pad_add_fusion.refs_0_, ...), custom_call_target="tpu_custom_call", output_to_operand_aliasing={{0}: (12, {}), {1}: (13, {}), {4}: (14, {}), {5}: (15, {})} | custom-call | flops 19999999655936 | bytes 10489856 | tf_op jit(solution)/shard_map/attend_back/pallas_call | solution.py:75
  319.5 10.1 %collective-permute-done.37.refs_3_ = bf16[512,512]{1,0:T(8,128)(2,1)S(1)} collective-permute-done((bf16[512,512]{1,0:T(8,128)(2,1)S(1)}, bf16[512,512]{1,0:T(8,128)(2,1)S(1)}, u32[]{:S(2)}, u32[]{:S(2)}) %collective-permute-start.37) | collective-permute-done | bytes 524320 | tf_op jit(solution)/shard_map/ppermute | solution.py:461
  335.5 24.6 %collective-permute-done.41 = bf16[512,1408]{1,0:T(8,128)(2,1)} collective-permute-done((bf16[512,1408]{1,0:T(8,128)(2,1)S(1)}, bf16[512,1408]{1,0:T(8,128)(2,1)}, u32[]{:S(2)}, u32[]{:S(2)}) %collective-permute-start.41) | collective-permute-done | bytes 1441824 | tf_op jit(solution)/shard_map/ppermute | solution.py:461
  363.8 6.4 %collective-permute-done.42.refs_4_ = bf16[256,512]{1,0:T(8,128)(2,1)S(1)} collective-permute-done((bf16[256,512]{1,0:T(8,128)(2,1)S(1)}, bf16[256,512]{1,0:T(8,128)(2,1)S(1)}, u32[]{:S(2)}, u32[]{:S(2)}) %collective-permute-start.42) | collective-permute-done | bytes 262176 | tf_op jit(solution)/shard_map/ppermute | solution.py:461
  373.1 7.2 %grad.9 = (bf16[2048,256]{1,0:T(8,128)(2,1)}, bf16[2048,256]{1,0:T(8,128)(2,1)}) custom-call(s32[4]{0:T(128)} %add_add_fusion.1.refs_0_, bf16[512,1024]{1,0:T(8,128)(2,1)} %get-tuple-element.185.refs_1_, bf16[512,1024]{1,0:T(8,128)(2,1)} %collective-permute-done.13.refs_2_, bf16[512,2048]{1,0:T(8,128)(2,1)} %get-tuple-element.247.refs_3_.refs_6_, ...), custom_call_target="tpu_custom_call" | custom-call | flops 9000000159744 | bytes 6291456 | tf_op jit(solution)/shard_map/grad/pallas_call | solution.py:75
  383.8 13.7 %collective-permute-done.44.refs_3_ = bf16[128,1024]{1,0:T(8,128)(2,1)} collective-permute-done((bf16[128,1024]{1,0:T(8,128)(2,1)}, bf16[128,1024]{1,0:T(8,128)(2,1)}, u32[]{:S(2)}, u32[]{:S(2)}) %collective-permute-start.44) | collective-permute-done | bytes 262176 | tf_op jit(solution)/shard_map/ppermute | solution.py:461
  397.5 3.1 latent_back.1
  401.1 5.9 %grad.10 = (bf16[256,1024]{1,0:T(8,128)(2,1)}, bf16[256,1024]{1,0:T(8,128)(2,1)}) custom-call(s32[4]{0:T(128)} %add_add_fusion.refs_0_, bf16[512,1024]{1,0:T(8,128)(2,1)} %get-tuple-element.170.refs_1_, bf16[512,1024]{1,0:T(8,128)(2,1)} %copy-done.43, bf16[512,1024]{1,0:T(8,128)(2,1)} %get-tuple-element.256.refs_3_, ...), custom_call_target="tpu_custom_call" | custom-call | flops 9000000159744 | bytes 4194304 | tf_op jit(solution)/shard_map/grad/pallas_call | solution.py:75
  407.0 7.3 %collective-permute-done.48.refs_3_ = bf16[128,2048]{1,0:T(8,128)(2,1)} collective-permute-done((bf16[128,2048]{1,0:T(8,128)(2,1)}, bf16[128,2048]{1,0:T(8,128)(2,1)}, u32[]{:S(2)}, u32[]{:S(2)}) %collective-permute-start.48) | collective-permute-done | bytes 524320 | tf_op jit(solution)/shard_map/ppermute | solution.py:461
  414.4 3.4 kv_split.1
  417.8 3.8 ffn_sum.1
  439.3 18.2 %collective-permute-done.52.refs_3_ = bf16[128,512]{1,0:T(8,128)(2,1)S(1)} collective-permute-done((bf16[128,512]{1,0:T(8,128)(2,1)S(1)}, bf16[128,512]{1,0:T(8,128)(2,1)S(1)}, u32[]{:S(2)}, u32[]{:S(2)}) %collective-permute-start.52) | collective-permute-done | bytes 131104 | tf_op jit(solution)/shard_map/ppermute | solution.py:461
  473.3 3.0 collective-permute-done.57
  478.4 3.5 join.1
  487.3 5.7 %grad.11 = (bf16[512,384]{1,0:T(8,128)(2,1)}, bf16[512,384]{1,0:T(8,128)(2,1)}) custom-call(s32[4]{0:T(128)} %add_add_fusion.refs_0_, bf16[512,2048]{1,0:T(8,128)(2,1)} %get-tuple-element.161.refs_1_, bf16[512,2048]{1,0:T(8,128)(2,1)} %collective-permute-done.1.refs_2_, bf16[512,384]{1,0:T(8,128)(2,1)} %get-tuple-element.278.refs_3_, bf16[512,384]{1,0:T(8,128)(2,1)} %copy-done.47), custom_call_target="tpu_custom_call" | custom-call | flops 9000000159744 | bytes 4980736 | tf_op jit(solution)/shard_map/grad/pallas_call | solution.py:75
  493.1 8.0 %input.2 = (bf16[2,256,2048]{2,1,0:T(8,128)(2,1)}, f32[1,2048]{1,0:T(1,128)}) custom-call(s32[3]{0:T(128)} %pad_add_fusion.refs_0_, bf16[512,1024]{1,0:T(8,128)(2,1)} %get-tuple-element.284.refs_1_, bf16[512,512]{1,0:T(8,128)(2,1)} %get-tuple-element.285.refs_2_, bf16[2,256,2048]{2,1,0:T(8,128)(2,1)} %refs_3_.9, bf16[2048,1024]{1,0:T(8,128)(2,1)} %refs_4_.9, ...), custom_call_target="tpu_custom_call" | custom-call | flops 7999999967232 | bytes 12066816 | tf_op jit(solution)/shard_map/input/pallas_call | solution.py:75
  504.6 8.0 %input.3 = (bf16[2,256,2048]{2,1,0:T(8,128)(2,1)}, f32[1,2048]{1,0:T(1,128)}) custom-call(s32[3]{0:T(128)} %pad_add_fusion.refs_0_, bf16[512,1024]{1,0:T(8,128)(2,1)} %get-tuple-element.284.refs_1_, bf16[512,512]{1,0:T(8,128)(2,1)} %get-tuple-element.285.refs_2_, bf16[2,256,2048]{2,1,0:T(8,128)(2,1)} %refs_3_.9, ...), custom_call_target="tpu_custom_call", output_to_operand_aliasing={{0}: (8, {})} | custom-call | flops 7999999967232 | bytes 12066816 | tf_op jit(solution)/shard_map/input/pallas_call | solution.py:75
  518.8 3.3 collective-permute-done.68
  522.1 3.1 collective-permute-start.69
  547.5 10.6 %collective-permute-done.65.refs_2_ = bf16[256,2048]{1,0:T(8,128)(2,1)S(1)} collective-permute-done((bf16[256,2048]{1,0:T(8,128)(2,1)}, bf16[256,2048]{1,0:T(8,128)(2,1)S(1)}, u32[]{:S(2)}, u32[]{:S(2)}) %collective-permute-start.65) | collective-permute-done | bytes 1048608 | tf_op jit(solution)/shard_map/ppermute | solution.py:461
  559.0 3.7 spread.1
  563.9 3.1 shared.1
  (303 shorter events, 154.9 us)
Async XLA Ops:
  9.1 16.8 %collective-permute-start.2 = (bf16[256,512]{1,0:T(8,128)(2,1)}, bf16[256,512]{1,0:T(8,128)(2,1)}, u32[]{:S(2)}, u32[]{:S(2)}) collective-permute-start(bf16[256,512]{1,0:T(8,128)(2,1)} %get-tuple-element.163), channel_id=1, source_target_pairs={{0,8},{4,12},{8,0},{12,4},{16,24},{20,28},{24,16},{28,20},{1,9},{5... | collective-permute-start | bytes 786440 | tf_op jit(solution)/shard_map/ppermute | solution.py:461
  37.0 20.9 %collective-permute-start.6 = (bf16[512,1024]{1,0:T(8,128)(2,1)}, bf16[512,1024]{1,0:T(8,128)(2,1)S(1)}, u32[]{:S(2)}, u32[]{:S(2)}) collective-permute-start(bf16[512,1024]{1,0:T(8,128)(2,1)} %get-tuple-element.170.refs_1_), channel_id=1, source_target_pairs={{0,4},{4,0},{8,12},{12,8},{16,20},{20,16},{24,28},{28,24},{1,5},{5... | collective-permute-start | bytes 3145736 | tf_op jit(solution)/shard_map/ppermute | solution.py:461
  58.0 19.4 %collective-permute-start.8 = (bf16[1024,512]{1,0:T(8,128)(2,1)}, bf16[1024,512]{1,0:T(8,128)(2,1)}, u32[]{:S(2)}, u32[]{:S(2)}) collective-permute-start(bf16[1024,512]{1,0:T(8,128)(2,1)} %constant_dynamic-update-slice_fusion.6.refs_3_.refs_5_), channel_id=1, source_target_pairs={{0,4},{4,0},{8,12},{12,8},{16,20},{20,16},{24,28},{28,24},{1,5},{5... | collective-permute-start | bytes 3145736 | tf_op jit(solution)/shard_map/ppermute | solution.py:461
  72.9 18.4 %collective-permute-start.10 = (bf16[64,2048]{1,0:T(8,128)(2,1)}, bf16[64,2048]{1,0:T(8,128)(2,1)}, u32[]{:S(2)}, u32[]{:S(2)}) collective-permute-start(bf16[64,2048]{1,0:T(8,128)(2,1)} %get-tuple-element.181), channel_id=1, source_target_pairs={{0,1},{1,0},{2,3},{3,2},{4,5},{5,4},{6,7},{7,6},{8,9},{9,8},{10,11... | collective-permute-start | bytes 786440 | tf_op jit(solution)/shard_map/ppermute | solution.py:461
  74.6 21.6 %collective-permute-start.11 = (bf16[64,2048]{1,0:T(8,128)(2,1)}, bf16[64,2048]{1,0:T(8,128)(2,1)}, u32[]{:S(2)}, u32[]{:S(2)}) collective-permute-start(bf16[64,2048]{1,0:T(8,128)(2,1)} %get-tuple-element.182), channel_id=1, source_target_pairs={{0,2},{1,3},{2,0},{3,1},{4,6},{5,7},{6,4},{7,5},{8,10},{9,11},{10,... | collective-permute-start | bytes 786440 | tf_op jit(solution)/shard_map/ppermute | solution.py:461
  77.1 19.1 %collective-permute-start.12 = (bf16[64,2048]{1,0:T(8,128)(2,1)}, bf16[64,2048]{1,0:T(8,128)(2,1)}, u32[]{:S(2)}, u32[]{:S(2)}) collective-permute-start(bf16[64,2048]{1,0:T(8,128)(2,1)} %get-tuple-element.183), channel_id=1, source_target_pairs={{0,3},{1,2},{2,1},{3,0},{4,7},{5,6},{6,5},{7,4},{8,11},{9,10},{10,... | collective-permute-start | bytes 786440 | tf_op jit(solution)/shard_map/ppermute | solution.py:461
  90.5 16.8 %collective-permute-start.13 = (bf16[512,1024]{1,0:T(8,128)(2,1)}, bf16[512,1024]{1,0:T(8,128)(2,1)}, u32[]{:S(2)}, u32[]{:S(2)}) collective-permute-start(bf16[512,1024]{1,0:T(8,128)(2,1)} %get-tuple-element.185.refs_1_), channel_id=1, source_target_pairs={{0,4},{4,0},{8,12},{12,8},{16,20},{20,16},{24,28},{28,24},{1,5},{5... | collective-permute-start | bytes 3145736 | tf_op jit(solution)/shard_map/ppermute | solution.py:461
  90.6 16.7 %collective-permute-start.9 = (bf16[128,2048]{1,0:T(8,128)(2,1)}, bf16[128,2048]{1,0:T(8,128)(2,1)}, u32[]{:S(2)}, u32[]{:S(2)}) collective-permute-start(bf16[128,2048]{1,0:T(8,128)(2,1)} %get-tuple-element.177), channel_id=1, source_target_pairs={{0,1},{1,0},{2,3},{3,2},{4,5},{5,4},{6,7},{7,6},{8,9},{9,8},{10,11... | collective-permute-start | bytes 1572872 | tf_op jit(solution)/shard_map/ppermute | solution.py:461
  99.4 17.8 %collective-permute-start.14 = (bf16[64,2048]{1,0:T(8,128)(2,1)}, bf16[64,2048]{1,0:T(8,128)(2,1)S(1)}, u32[]{:S(2)}, u32[]{:S(2)}) collective-permute-start(bf16[64,2048]{1,0:T(8,128)(2,1)} %get-tuple-element.188.refs_1_), channel_id=1, source_target_pairs={{0,1},{1,0},{2,3},{3,2},{4,5},{5,4},{6,7},{7,6},{8,9},{9,8},{10,11... | collective-permute-start | bytes 786440 | tf_op jit(solution)/shard_map/ppermute | solution.py:461
  104.9 27.2 %collective-permute-start.15 = (bf16[64,2048]{1,0:T(8,128)(2,1)}, bf16[64,2048]{1,0:T(8,128)(2,1)S(1)}, u32[]{:S(2)}, u32[]{:S(2)}) collective-permute-start(bf16[64,2048]{1,0:T(8,128)(2,1)} %get-tuple-element.188.refs_1_), channel_id=1, source_target_pairs={{0,2},{1,3},{2,0},{3,1},{4,6},{5,7},{6,4},{7,5},{8,10},{9,11},{10,... | collective-permute-start | bytes 786440 | tf_op jit(solution)/shard_map/ppermute | solution.py:461
  105.9 26.2 %collective-permute-start.16 = (bf16[64,2048]{1,0:T(8,128)(2,1)}, bf16[64,2048]{1,0:T(8,128)(2,1)S(1)}, u32[]{:S(2)}, u32[]{:S(2)}) collective-permute-start(bf16[64,2048]{1,0:T(8,128)(2,1)} %get-tuple-element.188.refs_1_), channel_id=1, source_target_pairs={{0,3},{1,2},{2,1},{3,0},{4,7},{5,6},{6,5},{7,4},{8,11},{9,10},{10,... | collective-permute-start | bytes 786440 | tf_op jit(solution)/shard_map/ppermute | solution.py:461
  108.4 33.1 %collective-permute-start.17 = (bf16[64,2048]{1,0:T(8,128)(2,1)S(1)}, bf16[64,2048]{1,0:T(8,128)(2,1)S(1)}, u32[]{:S(2)}, u32[]{:S(2)}) collective-permute-start(bf16[64,2048]{1,0:T(8,128)(2,1)S(1)} %add_convert_fusion.12), channel_id=1, source_target_pairs={{0,2},{1,3},{2,0},{3,1},{4,6},{5,7},{6,4},{7,5},{8,10},{9,11},{10,... | collective-permute-start | bytes 786440 | tf_op jit(solution)/shard_map/ppermute | solution.py:461
  145.0 26.9 %collective-permute-start.18 = (bf16[64,2048]{1,0:T(8,128)(2,1)}, bf16[64,2048]{1,0:T(8,128)(2,1)}, u32[]{:S(2)}, u32[]{:S(2)}) collective-permute-start(bf16[64,2048]{1,0:T(8,128)(2,1)} %get-tuple-element.194.refs_1_), channel_id=1, source_target_pairs={{0,1},{1,0},{2,3},{3,2},{4,5},{5,4},{6,7},{7,6},{8,9},{9,8},{10,11... | collective-permute-start | bytes 786440 | tf_op jit(solution)/shard_map/ppermute | solution.py:461
  145.1 28.2 %collective-permute-start.19 = (bf16[64,2048]{1,0:T(8,128)(2,1)}, bf16[64,2048]{1,0:T(8,128)(2,1)}, u32[]{:S(2)}, u32[]{:S(2)}) collective-permute-start(bf16[64,2048]{1,0:T(8,128)(2,1)} %get-tuple-element.194.refs_1_), channel_id=1, source_target_pairs={{0,2},{1,3},{2,0},{3,1},{4,6},{5,7},{6,4},{7,5},{8,10},{9,11},{10,... | collective-permute-start | bytes 786440 | tf_op jit(solution)/shard_map/ppermute | solution.py:461
  148.2 25.1 %collective-permute-start.20 = (bf16[64,2048]{1,0:T(8,128)(2,1)}, bf16[64,2048]{1,0:T(8,128)(2,1)}, u32[]{:S(2)}, u32[]{:S(2)}) collective-permute-start(bf16[64,2048]{1,0:T(8,128)(2,1)} %get-tuple-element.194.refs_1_), channel_id=1, source_target_pairs={{0,3},{1,2},{2,1},{3,0},{4,7},{5,6},{6,5},{7,4},{8,11},{9,10},{10,... | collective-permute-start | bytes 786440 | tf_op jit(solution)/shard_map/ppermute | solution.py:461
  168.8 24.3 %collective-permute-start.22 = (bf16[64,2048]{1,0:T(8,128)(2,1)}, bf16[64,2048]{1,0:T(8,128)(2,1)}, u32[]{:S(2)}, u32[]{:S(2)}) collective-permute-start(bf16[64,2048]{1,0:T(8,128)(2,1)} %get-tuple-element.202), channel_id=1, source_target_pairs={{0,1},{1,0},{2,3},{3,2},{4,5},{5,4},{6,7},{7,6},{8,9},{9,8},{10,11... | collective-permute-start | bytes 786440 | tf_op jit(solution)/shard_map/ppermute | solution.py:461
  168.9 24.3 %collective-permute-start.23 = (bf16[64,2048]{1,0:T(8,128)(2,1)}, bf16[64,2048]{1,0:T(8,128)(2,1)}, u32[]{:S(2)}, u32[]{:S(2)}) collective-permute-start(bf16[64,2048]{1,0:T(8,128)(2,1)} %get-tuple-element.203), channel_id=1, source_target_pairs={{0,2},{1,3},{2,0},{3,1},{4,6},{5,7},{6,4},{7,5},{8,10},{9,11},{10,... | collective-permute-start | bytes 786440 | tf_op jit(solution)/shard_map/ppermute | solution.py:461
  171.9 21.2 %collective-permute-start.24 = (bf16[64,2048]{1,0:T(8,128)(2,1)}, bf16[64,2048]{1,0:T(8,128)(2,1)}, u32[]{:S(2)}, u32[]{:S(2)}) collective-permute-start(bf16[64,2048]{1,0:T(8,128)(2,1)} %get-tuple-element.204), channel_id=1, source_target_pairs={{0,3},{1,2},{2,1},{3,0},{4,7},{5,6},{6,5},{7,4},{8,11},{9,10},{10,... | collective-permute-start | bytes 786440 | tf_op jit(solution)/shard_map/ppermute | solution.py:461
  193.0 20.8 %collective-permute-start.25 = (bf16[3,512,1408]{2,1,0:T(8,128)(2,1)}, bf16[3,512,1408]{2,1,0:T(8,128)(2,1)}, u32[]{:S(2)}, u32[]{:S(2)}) collective-permute-start(bf16[3,512,1408]{2,1,0:T(8,128)(2,1)} %get-tuple-element.206.refs_1_.refs_3_), channel_id=1, source_target_pairs={{0,4},{4,0},{8,12},{12,8},{16,20},{20,16},{24,28},{28,24},{1,5},{5... | collective-permute-start | bytes 12976136 | tf_op jit(solution)/shard_map/ppermute | solution.py:461
  193.1 20.7 %collective-permute-start.21 = (bf16[128,2048]{1,0:T(8,128)(2,1)}, bf16[128,2048]{1,0:T(8,128)(2,1)}, u32[]{:S(2)}, u32[]{:S(2)}) collective-permute-start(bf16[128,2048]{1,0:T(8,128)(2,1)} %get-tuple-element.199), channel_id=1, source_target_pairs={{0,1},{1,0},{2,3},{3,2},{4,5},{5,4},{6,7},{7,6},{8,9},{9,8},{10,11... | collective-permute-start | bytes 1572872 | tf_op jit(solution)/shard_map/ppermute | solution.py:461
  196.7 43.1 %collective-permute-start.28 = (bf16[64,2048]{1,0:T(8,128)(2,1)}, bf16[64,2048]{1,0:T(8,128)(2,1)}, u32[]{:S(2)}, u32[]{:S(2)}) collective-permute-start(bf16[64,2048]{1,0:T(8,128)(2,1)} %get-tuple-element.217.refs_2_), channel_id=1, source_target_pairs={{0,1},{1,0},{2,3},{3,2},{4,5},{5,4},{6,7},{7,6},{8,9},{9,8},{10,11... | collective-permute-start | bytes 786440 | tf_op jit(solution)/shard_map/ppermute | solution.py:461
  198.7 41.1 %collective-permute-start.29 = (bf16[64,2048]{1,0:T(8,128)(2,1)}, bf16[64,2048]{1,0:T(8,128)(2,1)}, u32[]{:S(2)}, u32[]{:S(2)}) collective-permute-start(bf16[64,2048]{1,0:T(8,128)(2,1)} %get-tuple-element.217.refs_2_), channel_id=1, source_target_pairs={{0,2},{1,3},{2,0},{3,1},{4,6},{5,7},{6,4},{7,5},{8,10},{9,11},{10,... | collective-permute-start | bytes 786440 | tf_op jit(solution)/shard_map/ppermute | solution.py:461
  199.7 40.0 %collective-permute-start.30 = (bf16[64,2048]{1,0:T(8,128)(2,1)}, bf16[64,2048]{1,0:T(8,128)(2,1)}, u32[]{:S(2)}, u32[]{:S(2)}) collective-permute-start(bf16[64,2048]{1,0:T(8,128)(2,1)} %get-tuple-element.217.refs_2_), channel_id=1, source_target_pairs={{0,3},{1,2},{2,1},{3,0},{4,7},{5,6},{6,5},{7,4},{8,11},{9,10},{10,... | collective-permute-start | bytes 786440 | tf_op jit(solution)/shard_map/ppermute | solution.py:461
  215.5 21.0 %collective-permute-start.27 = (bf16[64,2048]{1,0:T(8,128)(2,1)}, bf16[64,2048]{1,0:T(8,128)(2,1)}, u32[]{:S(2)}, u32[]{:S(2)}) collective-permute-start(bf16[64,2048]{1,0:T(8,128)(2,1)} %add_convert_fusion.11), channel_id=1, source_target_pairs={{0,2},{1,3},{2,0},{3,1},{4,6},{5,7},{6,4},{7,5},{8,10},{9,11},{10,... | collective-permute-start | bytes 786440 | tf_op jit(solution)/shard_map/ppermute | solution.py:461
  224.3 35.7 %collective-permute-start.32 = (bf16[2816,256]{1,0:T(8,128)(2,1)}, bf16[2816,256]{1,0:T(8,128)(2,1)}, u32[]{:S(2)}, u32[]{:S(2)}) collective-permute-start(bf16[2816,256]{1,0:T(8,128)(2,1)} %get-tuple-element.222), channel_id=1, source_target_pairs={{0,16},{4,20},{8,24},{12,28},{16,0},{20,4},{24,8},{28,12},{1,17},{... | collective-permute-start | bytes 4325384 | tf_op jit(solution)/shard_map/ppermute | solution.py:461
  239.8 21.7 %collective-permute-start.33 = (bf16[64,2048]{1,0:T(8,128)(2,1)}, bf16[64,2048]{1,0:T(8,128)(2,1)}, u32[]{:S(2)}, u32[]{:S(2)}) collective-permute-start(bf16[64,2048]{1,0:T(8,128)(2,1)} %get-tuple-element.223), channel_id=1, source_target_pairs={{0,2},{1,3},{2,0},{3,1},{4,6},{5,7},{6,4},{7,5},{8,10},{9,11},{10,... | collective-permute-start | bytes 786440 | tf_op jit(solution)/shard_map/ppermute | solution.py:461
  260.1 34.3 %collective-permute-start.34 = (bf16[512,1408]{1,0:T(8,128)(2,1)}, bf16[512,1408]{1,0:T(8,128)(2,1)}, u32[]{:S(2)}, u32[]{:S(2)}) collective-permute-start(bf16[512,1408]{1,0:T(8,128)(2,1)} %get-tuple-element.228), channel_id=1, source_target_pairs={{0,8},{4,12},{8,0},{12,4},{16,24},{20,28},{24,16},{28,20},{1,9},{5... | collective-permute-start | bytes 4325384 | tf_op jit(solution)/shard_map/ppermute | solution.py:461
  263.1 31.3 %collective-permute-start.35 = (bf16[128,2048]{1,0:T(8,128)(2,1)}, bf16[128,2048]{1,0:T(8,128)(2,1)}, u32[]{:S(2)}, u32[]{:S(2)}) collective-permute-start(bf16[128,2048]{1,0:T(8,128)(2,1)} %constant_dynamic-update-slice_fusion.8.refs_2_), channel_id=1, source_target_pairs={{0,1},{1,0},{2,3},{3,2},{4,5},{5,4},{6,7},{7,6},{8,9},{9,8},{10,11... | collective-permute-start | bytes 1572872 | tf_op jit(solution)/shard_map/ppermute | solution.py:461
  276.2 54.8 %collective-permute-start.38 = (bf16[256,2048]{1,0:T(8,128)(2,1)}, bf16[256,2048]{1,0:T(8,128)(2,1)}, u32[]{:S(2)}, u32[]{:S(2)}) collective-permute-start(bf16[256,2048]{1,0:T(8,128)(2,1)} %get-tuple-element.237), channel_id=1, source_target_pairs={{0,1},{1,0},{2,3},{3,2},{4,5},{5,4},{6,7},{7,6},{8,9},{9,8},{10,11... | collective-permute-start | bytes 3145736 | tf_op jit(solution)/shard_map/ppermute | solution.py:461
  314.7 16.2 %collective-permute-start.36 = (bf16[1024,512]{1,0:T(8,128)(2,1)}, bf16[1024,512]{1,0:T(8,128)(2,1)S(1)}, u32[]{:S(2)}, u32[]{:S(2)}) collective-permute-start(bf16[1024,512]{1,0:T(8,128)(2,1)} %get-tuple-element.233), channel_id=1, source_target_pairs={{0,4},{4,0},{8,12},{12,8},{16,20},{20,16},{24,28},{28,24},{1,5},{5... | collective-permute-start | bytes 3145736 | tf_op jit(solution)/shard_map/ppermute | solution.py:461
  315.6 44.5 %collective-permute-start.41 = (bf16[512,1408]{1,0:T(8,128)(2,1)S(1)}, bf16[512,1408]{1,0:T(8,128)(2,1)}, u32[]{:S(2)}, u32[]{:S(2)}) collective-permute-start(bf16[512,1408]{1,0:T(8,128)(2,1)S(1)} %copy-done.42), channel_id=1, source_target_pairs={{0,16},{4,20},{8,24},{12,28},{16,0},{20,4},{24,8},{28,12},{1,17},{... | collective-permute-start | bytes 4325384 | tf_op jit(solution)/shard_map/ppermute | solution.py:461
  316.9 43.2 %collective-permute-start.40 = (bf16[256,1024]{1,0:T(8,128)(2,1)}, bf16[256,1024]{1,0:T(8,128)(2,1)S(1)}, u32[]{:S(2)}, u32[]{:S(2)}) collective-permute-start(bf16[256,1024]{1,0:T(8,128)(2,1)} %get-tuple-element.240), channel_id=1, source_target_pairs={{0,1},{1,0},{2,3},{3,2},{4,5},{5,4},{6,7},{7,6},{8,9},{9,8},{10,11... | collective-permute-start | bytes 1572872 | tf_op jit(solution)/shard_map/ppermute | solution.py:461
  362.3 18.8 %collective-permute-start.39 = (bf16[512,512]{1,0:T(8,128)(2,1)}, bf16[512,512]{1,0:T(8,128)(2,1)}, u32[]{:S(2)}, u32[]{:S(2)}) collective-permute-start(bf16[512,512]{1,0:T(8,128)(2,1)} %add_convert_fusion.5), channel_id=1, source_target_pairs={{0,8},{4,12},{8,0},{12,4},{16,24},{20,28},{24,16},{28,20},{1,9},{5... | collective-permute-start | bytes 1572872 | tf_op jit(solution)/shard_map/ppermute | solution.py:461
  370.2 27.3 %collective-permute-start.44 = (bf16[128,1024]{1,0:T(8,128)(2,1)}, bf16[128,1024]{1,0:T(8,128)(2,1)}, u32[]{:S(2)}, u32[]{:S(2)}) collective-permute-start(bf16[128,1024]{1,0:T(8,128)(2,1)} %bitcast.12), channel_id=1, source_target_pairs={{0,2},{1,3},{2,0},{3,1},{4,6},{5,7},{6,4},{7,5},{8,10},{9,11},{10,... | collective-permute-start | bytes 786440 | tf_op jit(solution)/shard_map/ppermute | solution.py:461
  373.1 41.3 %collective-permute-start.48 = (bf16[128,2048]{1,0:T(8,128)(2,1)}, bf16[128,2048]{1,0:T(8,128)(2,1)}, u32[]{:S(2)}, u32[]{:S(2)}) collective-permute-start(bf16[128,2048]{1,0:T(8,128)(2,1)} %bitcast.13), channel_id=1, source_target_pairs={{0,2},{1,3},{2,0},{3,1},{4,6},{5,7},{6,4},{7,5},{8,10},{9,11},{10,... | collective-permute-start | bytes 1572872 | tf_op jit(solution)/shard_map/ppermute | solution.py:461
  383.0 31.4 %collective-permute-start.49 = (bf16[256,512]{1,0:T(8,128)(2,1)}, bf16[256,512]{1,0:T(8,128)(2,1)}, u32[]{:S(2)}, u32[]{:S(2)}) collective-permute-start(bf16[256,512]{1,0:T(8,128)(2,1)} %add_convert_fusion.8), channel_id=1, source_target_pairs={{0,16},{4,20},{8,24},{12,28},{16,0},{20,4},{24,8},{28,12},{1,17},{... | collective-permute-start | bytes 786440 | tf_op jit(solution)/shard_map/ppermute | solution.py:461
  383.8 17.4 %collective-permute-start.45 = (bf16[512,1024]{1,0:T(8,128)(2,1)}, bf16[512,1024]{1,0:T(8,128)(2,1)}, u32[]{:S(2)}, u32[]{:S(2)}) collective-permute-start(bf16[512,1024]{1,0:T(8,128)(2,1)} %get-tuple-element.256.refs_3_), channel_id=1, source_target_pairs={{0,4},{4,0},{8,12},{12,8},{16,20},{20,16},{24,28},{28,24},{1,5},{5... | collective-permute-start | bytes 3145736 | tf_op jit(solution)/shard_map/ppermute | solution.py:461
  400.6 21.7 %collective-permute-start.50 = (bf16[128,1024]{1,0:T(8,128)(2,1)}, bf16[128,1024]{1,0:T(8,128)(2,1)}, u32[]{:S(2)}, u32[]{:S(2)}) collective-permute-start(bf16[128,1024]{1,0:T(8,128)(2,1)} %get-tuple-element.264), channel_id=1, source_target_pairs={{0,2},{1,3},{2,0},{3,1},{4,6},{5,7},{6,4},{7,5},{8,10},{9,11},{10,... | collective-permute-start | bytes 786440 | tf_op jit(solution)/shard_map/ppermute | solution.py:461
  400.6 26.9 %collective-permute-start.47 = (bf16[2048,256]{1,0:T(8,128)(2,1)}, bf16[2048,256]{1,0:T(8,128)(2,1)}, u32[]{:S(2)}, u32[]{:S(2)}) collective-permute-start(bf16[2048,256]{1,0:T(8,128)(2,1)} %get-tuple-element.258), channel_id=1, source_target_pairs={{0,8},{4,12},{8,0},{12,4},{16,24},{20,28},{24,16},{28,20},{1,9},{5... | collective-permute-start | bytes 3145736 | tf_op jit(solution)/shard_map/ppermute | solution.py:461
  424.1 53.6 %collective-permute-start.60 = (bf16[256,1024]{1,0:T(8,128)(2,1)}, bf16[256,1024]{1,0:T(8,128)(2,1)}, u32[]{:S(2)}, u32[]{:S(2)}) collective-permute-start(bf16[256,1024]{1,0:T(8,128)(2,1)} %constant_dynamic-update-slice_fusion.10.refs_1_), channel_id=1, source_target_pairs={{0,1},{1,0},{2,3},{3,2},{4,5},{5,4},{6,7},{7,6},{8,9},{9,8},{10,11... | collective-permute-start | bytes 1572872 | tf_op jit(solution)/shard_map/ppermute | solution.py:461
  426.9 35.9 %collective-permute-start.54 = (bf16[128,2048]{1,0:T(8,128)(2,1)}, bf16[128,2048]{1,0:T(8,128)(2,1)}, u32[]{:S(2)}, u32[]{:S(2)}) collective-permute-start(bf16[128,2048]{1,0:T(8,128)(2,1)} %ffn_sum.1), channel_id=1, source_target_pairs={{0,2},{1,3},{2,0},{3,1},{4,6},{5,7},{6,4},{7,5},{8,10},{9,11},{10,... | collective-permute-start | bytes 1572872 | tf_op jit(solution)/shard_map/ppermute | solution.py:461
  428.4 29.0 %collective-permute-start.52 = (bf16[128,512]{1,0:T(8,128)(2,1)S(1)}, bf16[128,512]{1,0:T(8,128)(2,1)S(1)}, u32[]{:S(2)}, u32[]{:S(2)}) collective-permute-start(bf16[128,512]{1,0:T(8,128)(2,1)S(1)} %bitcast.35), channel_id=1, source_target_pairs={{0,2},{1,3},{2,0},{3,1},{4,6},{5,7},{6,4},{7,5},{8,10},{9,11},{10,... | collective-permute-start | bytes 393224 | tf_op jit(solution)/shard_map/ppermute | solution.py:461
  433.0 27.7 %collective-permute-start.53 = (bf16[1408,256]{1,0:T(8,128)(2,1)}, bf16[1408,256]{1,0:T(8,128)(2,1)}, u32[]{:S(2)}, u32[]{:S(2)}) collective-permute-start(bf16[1408,256]{1,0:T(8,128)(2,1)} %add_convert_fusion.2), channel_id=1, source_target_pairs={{0,8},{4,12},{8,0},{12,4},{16,24},{20,28},{24,16},{28,20},{1,9},{5... | collective-permute-start | bytes 2162696 | tf_op jit(solution)/shard_map/ppermute | solution.py:461
  438.7 29.9 %collective-permute-start.56 = (bf16[256,1408]{1,0:T(8,128)(2,1)}, bf16[256,1408]{1,0:T(8,128)(2,1)}, u32[]{:S(2)}, u32[]{:S(2)}) collective-permute-start(bf16[256,1408]{1,0:T(8,128)(2,1)} %add_convert_fusion.1), channel_id=1, source_target_pairs={{0,16},{4,20},{8,24},{12,28},{16,0},{20,4},{24,8},{28,12},{1,17},{... | collective-permute-start | bytes 2162696 | tf_op jit(solution)/shard_map/ppermute | solution.py:461
  528.6 29.4 %collective-permute-start.65 = (bf16[256,2048]{1,0:T(8,128)(2,1)}, bf16[256,2048]{1,0:T(8,128)(2,1)S(1)}, u32[]{:S(2)}, u32[]{:S(2)}) collective-permute-start(bf16[256,2048]{1,0:T(8,128)(2,1)} %constant_dynamic-update-slice_fusion.14.refs_1_), channel_id=1, source_target_pairs={{0,1},{1,0},{2,3},{3,2},{4,5},{5,4},{6,7},{7,6},{8,9},{9,8},{10,11... | collective-permute-start | bytes 3145736 | tf_op jit(solution)/shard_map/ppermute | solution.py:461
  536.3 26.3 %collective-permute-start.71 = (bf16[256,384]{1,0:T(8,128)(2,1)}, bf16[256,384]{1,0:T(8,128)(2,1)}, u32[]{:S(2)}, u32[]{:S(2)}) collective-permute-start(bf16[256,384]{1,0:T(8,128)(2,1)} %convert_add_fusion.5.refs_1_), channel_id=1, source_target_pairs={{0,1},{1,0},{2,3},{3,2},{4,5},{5,4},{6,7},{7,6},{8,9},{9,8},{10,11... | collective-permute-start | bytes 589832 | tf_op jit(solution)/shard_map/ppermute | solution.py:461
  538.0 24.7 %collective-permute-start.72 = (bf16[256,384]{1,0:T(8,128)(2,1)}, bf16[256,384]{1,0:T(8,128)(2,1)}, u32[]{:S(2)}, u32[]{:S(2)}) collective-permute-start(bf16[256,384]{1,0:T(8,128)(2,1)} %convert_add_fusion.5.refs_1_), channel_id=1, source_target_pairs={{0,2},{1,3},{2,0},{3,1},{4,6},{5,7},{6,4},{7,5},{8,10},{9,11},{10,... | collective-permute-start | bytes 589832 | tf_op jit(solution)/shard_map/ppermute | solution.py:461
  539.2 24.8 %collective-permute-start.73 = (bf16[256,384]{1,0:T(8,128)(2,1)}, bf16[256,384]{1,0:T(8,128)(2,1)}, u32[]{:S(2)}, u32[]{:S(2)}) collective-permute-start(bf16[256,384]{1,0:T(8,128)(2,1)} %convert_add_fusion.5.refs_1_), channel_id=1, source_target_pairs={{0,3},{1,2},{2,1},{3,0},{4,7},{5,6},{6,5},{7,4},{8,11},{9,10},{10,... | collective-permute-start | bytes 589832 | tf_op jit(solution)/shard_map/ppermute | solution.py:461
  (81 other events, 849.6 us)
